TPU v7x, 32 devices: a whole 2x2x4 slice. The times are simulated.
32 devices in a mesh: col: 2 (over core), dev: 16 (over z, y, x).
Axes of the slice: x: 2, y: 2, z: 4, core: 2. Of those that a mesh axis runs over, the one named last changes fastest.
Arguments:
- factor_a: float32 [1536, 16, 512], P('dev'), may hold values from -1 to 1
- factor_b: float32 [1536, 64, 512], P('dev', 'col'), may hold values from -1 to 1
- factor_occ: float32 [1536, 16, 512], P('dev'), may hold values from -1 to 1
- singles_a: float32 [16, 16], replicated, may hold values from -1.5 to 1.5
- singles_b: float32 [16, 64], P(None, 'col'), may hold values from -1.5 to 1.5
- doubles: bfloat16 [512, 512, 256], P('col', 'dev'), may hold values from -0.023925781 to 0.023925781
- orbital_a: float32 [16], P('col'), may hold values from 0.2 to 3
- orbital_b: float32 [64], P('dev'), may hold values from 0.2 to 3
- orbital_occ: float32 [16], replicated, may hold values from -2 to -0.3
Outputs:
- update: float32 [16, 64, 256], P('col', 'dev')
All inputs are finite; a program needn't handle non-finite values.
Results may differ from a plain program's by a relative error of at most 0.0049.
Values may be sent and summed in bfloat16 or wider, within the bound.
No kernel may reach another device: no remote copies, remote signals or barrier semaphores. Data moves between devices by JAX's collectives and lax.ppermute only.
A program may use at most 128 MiB of HBM per device.

v0:
```python
import functools

import jax
import jax.numpy as jnp
from jax import lax
from jax.experimental import pallas as pl
from jax.experimental.pallas import tpu as pltpu
from jax.sharding import PartitionSpec as P


F32 = jnp.float32
BF16 = jnp.bfloat16
LANES = 128
TALL = 16
GROUP = 4
CHAIN = 4


def params(n):
    return pltpu.CompilerParams(
        dimension_semantics=("arbitrary",) * n, vmem_limit_bytes=60 * 1024 * 1024
    )


def split(value, size):
    return jnp.right_shift(value, size.bit_length() - 1), jnp.bitwise_and(value, size - 1)


def reorder(inner, outer, shift=0):
    n = inner * outer
    row = lax.broadcasted_iota(jnp.int32, (n, 1), 0)
    column = lax.broadcasted_iota(jnp.int32, (1, n), 1)
    o, i = split(row, inner)
    source = i * outer + split(o + shift, outer)[1]
    return jnp.where(column == source, 1.0, 0.0).astype(BF16)


def halves_of(value):
    high = value.astype(BF16)
    return high, (value - high.astype(F32)).astype(BF16)


def spread(singles, q_rows):
    occ, rows = singles.shape
    exact = dict(precision=lax.Precision.HIGHEST, preferred_element_type=F32)
    high, wide = q_rows * rows, q_rows * occ
    row_q, row = split(lax.broadcasted_iota(jnp.int32, (high, 1), 0), rows)
    column_q, column = split(lax.broadcasted_iota(jnp.int32, (1, wide), 1), occ)
    pick_row = jnp.where(row == lax.broadcasted_iota(jnp.int32, (high, rows), 1), 1.0, 0.0)
    pick_k = jnp.where(column == lax.broadcasted_iota(jnp.int32, (occ, wide), 0), 1.0, 0.0)
    value = lax.dot_general(pick_row, singles, (((1,), (1,)), ((), ())), **exact)
    value = jnp.dot(value, pick_k, **exact)
    first, second = halves_of(jnp.where(row_q == column_q, value, 0.0))
    return jnp.concatenate([first, first, second], axis=1)


def dressed(factors, occ, mix_ref, order_ref):
    first, second = halves_of(occ)
    parts = jnp.concatenate([first, second, first], axis=0)
    change = jnp.dot(mix_ref[...], parts, preferred_element_type=F32)
    value = (factors - change).astype(BF16)
    return jnp.dot(order_ref[...], value, preferred_element_type=F32)


def swap_kernel(t_ref, o_ref, order):
    d_rows = t_ref.shape[1]

    @pl.when(pl.program_id(0) == 0)
    def _():
        order[...] = reorder(TALL, d_rows)

    for start in range(0, t_ref.shape[0], TALL):
        flat = t_ref[start : start + TALL].reshape(TALL * d_rows, t_ref.shape[2])
        value = jnp.dot(order[...], flat, preferred_element_type=F32).astype(BF16)
        for d in range(d_rows):
            o_ref[d, start : start + TALL, :] = value[d * TALL : (d + 1) * TALL]


def swap_doubles(doubles):
    c_tile, d_tile, pairs = doubles.shape
    rows = 4 * TALL
    return pl.pallas_call(
        swap_kernel,
        out_shape=jax.ShapeDtypeStruct((d_tile, c_tile, pairs), BF16),
        grid=(c_tile // rows,),
        in_specs=[pl.BlockSpec((rows, d_tile, pairs), lambda i: (i, 0, 0))],
        out_specs=pl.BlockSpec((d_tile, rows, pairs), lambda i: (0, i, 0)),
        scratch_shapes=[pltpu.VMEM((TALL * d_tile, TALL * d_tile), BF16)],
        compiler_params=params(1),
        cost_estimate=pl.CostEstimate(
            flops=0, bytes_accessed=4 * doubles.size, transcendentals=0
        ),
    )(doubles)


def dress_a_kernel(where, f_ref, occ_ref, singles_ref, out, mix, order):
    a_rows = f_ref.shape[0] // TALL
    width = f_ref.shape[1]

    @pl.when(pl.program_id(0) == 0)
    def _():
        mix[...] = spread(singles_ref[...], TALL)
        order[...] = reorder(TALL, a_rows, where[0] * (a_rows // 2))

    value = dressed(f_ref[...], occ_ref[...], mix, order).astype(BF16)
    for a in range(a_rows):
        out[:, a * width : (a + 1) * width] = value[a * TALL : (a + 1) * TALL]


def dress_a(col, factor_a, factor_occ, singles_a, c_tile):
    shard, a_rows, wide = factor_a.shape
    occ_rows = factor_occ.shape[1]
    columns = a_rows * c_tile
    return pl.pallas_call(
        dress_a_kernel,
        out_shape=jax.ShapeDtypeStruct((shard, columns), BF16),
        grid_spec=pltpu.PrefetchScalarGridSpec(
            num_scalar_prefetch=1,
            grid=(shard // TALL,),
            in_specs=[
                pl.BlockSpec((TALL * a_rows, c_tile), lambda i, w: (i, w[0])),
                pl.BlockSpec((TALL * occ_rows, c_tile), lambda i, w: (i, w[0])),
                pl.BlockSpec(singles_a.shape, lambda i, w: (0, 0)),
            ],
            out_specs=pl.BlockSpec((TALL, columns), lambda i, w: (i, 0)),
            scratch_shapes=[
                pltpu.VMEM((TALL * a_rows, 3 * TALL * occ_rows), BF16),
                pltpu.VMEM((TALL * a_rows, TALL * a_rows), BF16),
            ],
        ),
        compiler_params=params(1),
        cost_estimate=pl.CostEstimate(
            flops=2 * shard * a_rows * occ_rows * c_tile,
            bytes_accessed=10 * shard * a_rows * c_tile,
            transcendentals=0,
        ),
    )(
        col.reshape(1),
        factor_a.reshape(shard * a_rows, wide),
        factor_occ.reshape(shard * occ_rows, wide),
        singles_a,
    )


def dress_b_kernel(slots, where, *refs):
    pairs = slots // 2
    f_refs, occ_refs, singles_ref = refs[:pairs], refs[pairs : 2 * pairs], refs[2 * pairs]
    outs, (mix, order) = refs[2 * pairs + 1 : -2], refs[-2:]
    b_rows = f_refs[0].shape[0] // TALL

    @pl.when(pl.program_id(0) == 0)
    def _():
        mix[...] = spread(singles_ref[...], TALL)
        order[...] = reorder(TALL, b_rows)

    lane = lax.broadcasted_iota(jnp.int32, (TALL, LANES), 1)
    low_half = lane < LANES // 2
    even = jnp.bitwise_and(lane, LANES // GROUP) == 0
    swap_slot = lax.rem(where[0] // 2, 2) == 1
    swap_tile = lax.rem(where[0], 2) == 1

    def roll(v, n):
        return pltpu.roll(v, n % LANES, 1)

    both = dressed(
        jnp.concatenate([r[...] for r in f_refs], axis=1),
        jnp.concatenate([r[...] for r in occ_refs], axis=1),
        mix,
        order,
    )
    for pair in range(pairs):
        value = both[:, pair * LANES : (pair + 1) * LANES]
        for b in range(0, b_rows, GROUP):
            x0, x1, x2, x3 = (value[(b + i) * TALL : (b + i + 1) * TALL] for i in range(GROUP))
            half = LANES // 2
            low0 = jnp.where(low_half, x0, roll(x2, half))
            high0 = jnp.where(low_half, roll(x0, half), x2)
            low1 = jnp.where(low_half, x1, roll(x3, half))
            high1 = jnp.where(low_half, roll(x1, half), x3)
            step = LANES // GROUP
            y00 = jnp.where(even, low0, roll(low1, step))
            y01 = jnp.where(even, roll(low0, -step), low1)
            y10 = jnp.where(even, high0, roll(high1, step))
            y11 = jnp.where(even, roll(high0, -step), high1)
            p00, p10 = jnp.where(swap_slot, y10, y00), jnp.where(swap_slot, y00, y10)
            p01, p11 = jnp.where(swap_slot, y11, y01), jnp.where(swap_slot, y01, y11)
            r00, r01 = jnp.where(swap_tile, p01, p00), jnp.where(swap_tile, p00, p01)
            r10, r11 = jnp.where(swap_tile, p11, p10), jnp.where(swap_tile, p10, p11)
            at = slice(b * step, b * step + LANES)
            outs[2 * pair][:, at] = r00.astype(BF16)
            outs[2 * pair + 1][:, at] = r10.astype(BF16)
            outs[slots + 2 * pair][:, at] = r01.astype(BF16)
            outs[slots + 2 * pair + 1][:, at] = r11.astype(BF16)


def dress_b(dev, factor_b, factor_occ, singles_b, d_tile, slots):
    shard, b_rows, wide = factor_b.shape
    occ_rows = factor_occ.shape[1]
    pairs = slots // 2
    out = jax.ShapeDtypeStruct((shard, b_rows * d_tile), BF16)

    def windows(rows):
        return [
            pl.BlockSpec((TALL * rows, LANES), lambda i, w, p=p: (i, jnp.bitwise_xor(w[0] // 4, p)))
            for p in range(pairs)
        ]

    outs = pl.pallas_call(
        functools.partial(dress_b_kernel, slots),
        out_shape=[out] * (2 * slots),
        grid_spec=pltpu.PrefetchScalarGridSpec(
            num_scalar_prefetch=1,
            grid=(shard // TALL,),
            in_specs=windows(b_rows)
            + windows(occ_rows)
            + [pl.BlockSpec(singles_b.shape, lambda i, w: (0, 0))],
            out_specs=[pl.BlockSpec((TALL, out.shape[1]), lambda i, w: (i, 0))] * (2 * slots),
            scratch_shapes=[
                pltpu.VMEM((TALL * b_rows, 3 * TALL * occ_rows), BF16),
                pltpu.VMEM((TALL * b_rows, TALL * b_rows), BF16),
            ],
        ),
        compiler_params=params(1),
        cost_estimate=pl.CostEstimate(
            flops=2 * shard * b_rows * occ_rows * wide,
            bytes_accessed=8 * shard * b_rows * wide,
            transcendentals=0,
        ),
    )(
        dev.reshape(1),
        *[factor_b.reshape(shard * b_rows, wide)] * pairs,
        *[factor_occ.reshape(shard * occ_rows, wide)] * pairs,
        singles_b,
    )
    return outs[:slots], outs[slots:]


def turn_kernel(slots, d_tile, *refs):
    blocks, o_ref, order = refs[:slots], refs[slots], refs[slots + 1]

    @pl.when(pl.program_id(0) == 0)
    def _():
        order[...] = reorder(TALL, d_tile)

    tall = jnp.concatenate([r[...] for r in blocks], axis=0)
    value = lax.dot_general(
        order[...], tall, (((1,), (1,)), ((), ())), preferred_element_type=F32
    ).astype(BF16)
    for d in range(d_tile):
        o_ref[d] = value[d * TALL : (d + 1) * TALL]


def turn(blocks, d_tile):
    slots = len(blocks)
    shard, columns = blocks[0].shape
    width = TALL * d_tile
    depth = slots * shard
    return pl.pallas_call(
        functools.partial(turn_kernel, slots, d_tile),
        out_shape=jax.ShapeDtypeStruct((d_tile, columns // d_tile, depth), BF16),
        grid=(columns // width,),
        in_specs=[pl.BlockSpec((shard, width), lambda i: (0, i))] * slots,
        out_specs=pl.BlockSpec((d_tile, TALL, depth), lambda i: (0, i, 0)),
        scratch_shapes=[pltpu.VMEM((width, width), BF16)],
        compiler_params=params(1),
        cost_estimate=pl.CostEstimate(
            flops=0, bytes_accessed=4 * depth * columns, transcendentals=0
        ),
    )(*blocks)


def ladder_kernel(slots, chunks, has_start, *refs):
    n = slots * chunks
    a_refs, (own_ref, other_ref, t_ref) = refs[:n], refs[n : n + 3]
    refs = refs[n + 3 :]
    starts, refs = (refs[:2], refs[2:]) if has_start else ((), refs)
    keep_ref, send_ref, whole_a, integral, total, sems = refs
    step = pl.program_id(0)
    shard, width = a_refs[0].shape

    def copies():
        return [
            pltpu.make_async_copy(
                a_refs[c * slots + k],
                whole_a.at[pl.ds(k * shard, shard), pl.ds(c * width, width)],
                sems.at[c * slots + k],
            )
            for c in range(chunks)
            for k in range(slots)
        ]

    half = total.shape[0] // 2

    @pl.when(step == 0)
    def _():
        for copy in copies():
            copy.start()
        if has_start:
            total[:half, :] = starts[0][...]
            total[half:, :] = starts[1][...]
        else:
            total[...] = jnp.zeros_like(total)
        for copy in copies():
            copy.wait()

    d_rows, b_local, depth = own_ref.shape
    c_tile = t_ref.shape[1]
    b_all = 2 * b_local
    rows = jnp.concatenate([own_ref[...], other_ref[...]], axis=1)
    rows = rows.reshape(d_rows * b_all, depth)
    for a in range(whole_a.shape[1] // c_tile):
        value = jnp.dot(
            rows, whole_a[:, a * c_tile : (a + 1) * c_tile], preferred_element_type=F32
        ).astype(BF16)
        for d in range(d_rows):
            integral[a * b_all : (a + 1) * b_all, d * c_tile : (d + 1) * c_tile] = value[
                d * b_all : (d + 1) * b_all
            ]
    weights = t_ref[...].reshape(d_rows * c_tile, t_ref.shape[2])
    total[...] += jnp.dot(integral[...], weights, preferred_element_type=F32)

    @pl.when(step == pl.num_programs(0) - 1)
    def _():
        keep_ref[...] = total[:half, :]
        send_ref[...] = total[half:, :]


def ladder(a_blocks, own, other, doubles, starts, d_rows=8):
    chunks, slots = len(a_blocks), len(a_blocks[0])
    _, width = a_blocks[0][0].shape
    d_tile, b_local, depth = own.shape
    c_tile, pairs = doubles.shape[1:]
    columns = chunks * width
    a_rows = columns // c_tile
    rows = a_rows * 2 * b_local
    out = jax.ShapeDtypeStruct((rows // 2, pairs), F32)
    full = pl.BlockSpec((rows // 2, pairs), lambda i: (0, 0))
    return pl.pallas_call(
        functools.partial(ladder_kernel, slots, chunks, bool(starts)),
        out_shape=[out, out],
        grid=(d_tile // d_rows,),
        in_specs=[pl.BlockSpec(memory_space=pl.ANY)] * (chunks * slots)
        + [pl.BlockSpec((d_rows, b_local, depth), lambda i: (i, 0, 0))] * 2
        + [pl.BlockSpec((d_rows, c_tile, pairs), lambda i: (i, 0, 0))]
        + [full] * len(starts),
        out_specs=[full, full],
        scratch_shapes=[
            pltpu.VMEM((depth, columns), BF16),
            pltpu.VMEM((rows, d_rows * c_tile), BF16),
            pltpu.VMEM((rows, pairs), F32),
            pltpu.SemaphoreType.DMA((chunks * slots,)),
        ],
        compiler_params=params(1),
        cost_estimate=pl.CostEstimate(
            flops=2 * d_tile * 2 * b_local * columns * (depth + pairs),
            bytes_accessed=2 * depth * columns + 2 * doubles.size,
            transcendentals=0,
        ),
    )(*[b for chunk in a_blocks for b in chunk], own, other, doubles, *starts)


def exchange(value, bits, size):
    return lax.ppermute(value, "dev", [(d, d ^ bits) for d in range(size)])


def gated(value, *after):
    return lax.optimization_barrier((value,) + after)[0]


def plane_gather(block, size, link):
    low, high = 2 * link, 4 * link

    def chain(d):
        return (d // low) % CHAIN

    middle = [(d, d ^ (low | high)) for d in range(size) if chain(d) in (1, 2)]
    outward = [(d, d ^ low) for d in range(size) if chain(d) in (1, 2)]
    position = chain(lax.axis_index("dev"))
    inner = (position == 1) | (position == 2)
    near = exchange(block, low, size)
    mid_own = lax.ppermute(block, "dev", middle)
    mid_near = lax.ppermute(near, "dev", middle)
    out_own = lax.ppermute(mid_own, "dev", outward)
    out_near = lax.ppermute(mid_near, "dev", outward)
    far = jnp.where(inner, mid_near, out_own)
    farthest = jnp.where(inner, mid_own, out_near)
    found = []
    for part in (block, near, far, farthest):
        found += [part, exchange(part, link, size)]
    return found, (near, mid_near, out_own, far, farthest)


def fast_body(
    size,
    factor_a,
    factor_b,
    factor_occ,
    singles_a,
    singles_b,
    doubles,
    orbital_a,
    orbital_b,
    orbital_occ,
):
    c_tile, d_tile, pairs = doubles.shape
    a_rows, b_local = factor_a.shape[1], factor_b.shape[1]
    slots = size // 2
    col = lax.axis_index("col").astype(jnp.int32)
    dev = lax.axis_index("dev").astype(jnp.int32)
    block_a = dress_a(col, factor_a, factor_occ, singles_a, c_tile)
    mine = swap_doubles(doubles)
    theirs = exchange(mine, 1, size)
    whole_a, (near, mid_near, out_own, far, farthest) = plane_gather(block_a, size, 2)
    halves = dress_b(dev, factor_b, factor_occ, singles_b, d_tile, slots)
    partial_value = ()
    order = [slot for slot in (4, 6, 5, 7, 2, 3, 1) if slot < slots]
    for n, (half, weights) in enumerate(zip(halves, (mine, theirs))):
        found = {0: half[0]}
        for slot in order:
            if n:
                gate = farthest if slot in order[:2] else first[order[1]]
            else:
                gate = far if slot in order[:2] else farthest
            found[slot] = exchange(gated(half[slot], gate), 2 * slot, size)
        first = found
        own = turn([found[k] for k in range(slots)], d_tile)
        other = lax.ppermute(own, "col", [(0, 1), (1, 0)])
        partial_value = ladder([whole_a], own, other, weights, tuple(partial_value))
    keep, send = partial_value
    got = lax.ppermute(send, "col", [(0, 1), (1, 0)])
    a_half = a_rows // 2
    keep = keep.reshape(a_half, 2, b_local, pairs)
    got = got.reshape(a_half, 2, b_local, pairs)
    first = jnp.where(col == 0, keep[:, 0] + got[:, 1], keep[:, 1] + got[:, 0])
    second = jnp.where(col == 0, keep[:, 1] + got[:, 0], keep[:, 0] + got[:, 1])
    both = jnp.stack([first, second])
    b_own = 2 * b_local // size
    both = both.reshape(2, a_half, size // 2, b_own, pairs)
    both = jnp.transpose(both, (0, 2, 1, 3, 4)).reshape(size, a_half * b_own, pairs)
    moved = lax.all_to_all(both, "dev", split_axis=0, concat_axis=0, tiled=True)
    total = jnp.sum(moved, axis=0).reshape(a_half, b_own, pairs)
    pair_energy = (orbital_occ[:, None] + orbital_occ[None, :]).reshape(-1)
    denominator = orbital_a[:, None, None] + orbital_b[None, :, None] - pair_energy[None, None, :]
    return total / denominator


def plain_body(
    factor_a, factor_b, factor_occ, singles_a, singles_b, doubles, orbital_a, orbital_b, orbital_occ
):
    highest = lax.Precision.HIGHEST
    c_tile = doubles.shape[0]
    d_tile = doubles.shape[1]
    pair_count = doubles.shape[2]
    shard_rows = factor_a.shape[0]
    a_rows = factor_a.shape[1]
    b_local = factor_b.shape[1]
    d_groups = factor_b.shape[2] // d_tile
    col_index = lax.axis_index("col")
    occ_tile = lax.dynamic_slice_in_dim(factor_occ, col_index * c_tile, c_tile, 2)
    a_tile = lax.dynamic_slice_in_dim(factor_a, col_index * c_tile, c_tile, 2)
    dressed_a = (a_tile - jnp.einsum("ka,qkc->qac", singles_a, occ_tile, precision=highest)).astype(
        jnp.bfloat16
    )
    dressed_a = dressed_a.reshape(shard_rows, a_rows * c_tile)
    dressed_b = (
        factor_b - jnp.einsum("kb,qkd->qbd", singles_b, factor_occ, precision=highest)
    ).astype(jnp.bfloat16)
    grouped = dressed_b.reshape(shard_rows, b_local, d_groups, d_tile)
    grouped = jnp.transpose(grouped, (0, 2, 1, 3)).reshape(shard_rows, d_groups, b_local * d_tile)
    moved = lax.all_to_all(grouped, "dev", split_axis=1, concat_axis=0, tiled=True)
    collected = lax.all_gather(moved, "col", axis=1, tiled=True)
    whole_b = collected.reshape(collected.shape[0], -1)
    b_rows_all = whole_b.shape[1] // d_tile
    contract_first = (((0,), (0,)), ((), ()))
    whole_a = lax.all_gather(dressed_a, "dev", axis=0, tiled=True)
    integral = lax.dot_general(whole_a, whole_b, contract_first, preferred_element_type=jnp.float32)
    integral = integral.astype(jnp.bfloat16).reshape(a_rows, c_tile, b_rows_all, d_tile)
    integral = jnp.transpose(integral, (0, 2, 1, 3)).reshape(a_rows * b_rows_all, c_tile * d_tile)
    partial_value = jnp.dot(
        integral, doubles.reshape(c_tile * d_tile, pair_count), preferred_element_type=jnp.float32
    )
    partial_value = partial_value.reshape(a_rows, b_rows_all, pair_count)
    reduced = lax.psum_scatter(partial_value, "dev", scatter_dimension=1, tiled=True)
    total = lax.psum_scatter(reduced, "col", scatter_dimension=0, tiled=True)
    pair_energy = (orbital_occ[:, None] + orbital_occ[None, :]).reshape(-1)
    denominator = orbital_a[:, None, None] + orbital_b[None, :, None] - pair_energy[None, None, :]
    return total / denominator


def solution(mesh):
    size, columns = mesh.shape["dev"], mesh.shape["col"]

    def body(factor_a, factor_b, factor_occ, singles_a, singles_b, doubles, *orbitals):
        fits = (
            columns == 2
            and size == 4 * CHAIN
            and doubles.shape[1] * GROUP == LANES
            and doubles.shape[0] % LANES == 0
            and doubles.shape[2] % LANES == 0
            and factor_a.shape[0] % TALL == 0
            and factor_b.shape[1] % TALL == 0
        )
        chosen = functools.partial(fast_body, size) if fits else plain_body
        return chosen(factor_a, factor_b, factor_occ, singles_a, singles_b, doubles, *orbitals)

    return jax.shard_map(
        body,
        mesh=mesh,
        in_specs=(
            P("dev", None, None),
            P("dev", "col", None),
            P("dev", None, None),
            P(),
            P(None, "col"),
            P("col", "dev", None),
            P("col"),
            P("dev"),
            P(),
        ),
        out_specs=P("col", "dev", None),
        check_vma=False,
    )
```

profile of v0, /device:TPU:0, one launch (start us, length us, event | category | flops | bytes accessed | tf_op | source)
XLA Modules:
  0.0 269.4 jit_solution(15395717128677598709)
XLA Ops:
  0.0 6.8 %shard_map.91.refs_0_ = bf16[96,4096]{1,0:T(8,128)(2,1)} custom-call(s32[1]{0:T(128)} %bitcast.where, f32[1536,512]{1,0:T(8,128)} %bitcast.21, f32[1536,512]{1,0:T(8,128)} %bitcast.16, f32[16,16]{1,0:T(8,128)} %singles_ref.1), custom_call_target="tpu_custom_call" | custom-call | flops 12582912 | bytes 3932160 | tf_op jit(solution)/shard_map/pallas_call | solution.py:114
  6.8 3.1 %collective-permute-start.1 = (bf16[96,4096]{1,0:T(8,128)(2,1)}, bf16[96,4096]{1,0:T(8,128)(2,1)S(1)}, u32[]{:S(2)}, u32[]{:S(2)}) collective-permute-start(bf16[96,4096]{1,0:T(8,128)(2,1)} %shard_map.91.refs_0_), channel_id=1, source_target_pairs={{0,4},{1,5},{2,6},{3,7},{4,0},{5,1},{6,2},{7,3},{8,12},{9,13},{10,... | collective-permute-start | bytes 2359304 | tf_op jit(solution)/shard_map/ppermute | solution.py:363
  10.5 17.0 %collective-permute-done.1.refs_2_ = bf16[96,4096]{1,0:T(8,128)(2,1)S(1)} collective-permute-done((bf16[96,4096]{1,0:T(8,128)(2,1)}, bf16[96,4096]{1,0:T(8,128)(2,1)S(1)}, u32[]{:S(2)}, u32[]{:S(2)}) %collective-permute-start.1) | collective-permute-done | bytes 786464 | tf_op jit(solution)/shard_map/ppermute | solution.py:363
  31.3 6.2 %shard_map.94.refs_10_ = bf16[32,256,256]{2,1,0:T(8,128)(2,1)} custom-call(bf16[256,32,256]{2,1,0:T(8,128)(2,1)} %t_ref.1), custom_call_target="tpu_custom_call" | custom-call | bytes 8388608 | tf_op jit(solution)/shard_map/pallas_call | solution.py:82
  39.1 11.8 %shard_map.92 = (bf16[96,1024]{1,0:T(8,128)(2,1)}, bf16[96,1024]{1,0:T(8,128)(2,1)}, bf16[96,1024]{1,0:T(8,128)(2,1)}, bf16[96,1024]{1,0:T(8,128)(2,1)}, bf16[96...) custom-call(s32[1]{0:T(128)} %bitcast.3.where, ...), custom_call_target="tpu_custom_call" | custom-call | flops 50331648 | bytes 12582912 | tf_op jit(solution)/shard_map/pallas_call | solution.py:208
  52.7 5.2 %collective-permute-start.22 = (bf16[96,1024]{1,0:T(8,128)(2,1)}, bf16[96,1024]{1,0:T(8,128)(2,1)S(1)}, u32[]{:S(2)}, u32[]{:S(2)}) collective-permute-start(bf16[96,1024]{1,0:T(8,128)(2,1)} %get-tuple-element.64), channel_id=1, source_target_pairs={{0,8},{1,9},{2,10},{3,11},{4,12},{5,13},{6,14},{7,15},{8,0},{9,1},... | collective-permute-start | bytes 589832 | tf_op jit(solution)/shard_map/ppermute | solution.py:363
  59.6 21.5 %collective-permute-done.7 = bf16[96,4096]{1,0:T(8,128)(2,1)S(1)} collective-permute-done((bf16[96,4096]{1,0:T(8,128)(2,1)S(1)}, bf16[96,4096]{1,0:T(8,128)(2,1)S(1)}, u32[]{:S(2)}, u32[]{:S(2)}) %collective-permute-start.7) | collective-permute-done | bytes 786464 | tf_op jit(solution)/shard_map/ppermute | solution.py:384
  84.8 3.4 %collective-permute-done.19.refs_1_ = bf16[96,1024]{1,0:T(8,128)(2,1)S(1)} collective-permute-done((bf16[96,1024]{1,0:T(8,128)(2,1)S(1)}, bf16[96,1024]{1,0:T(8,128)(2,1)S(1)}, u32[]{:S(2)}, u32[]{:S(2)}) %collective-permute-start.19) | collective-permute-done | bytes 196640 | tf_op jit(solution)/shard_map/ppermute | solution.py:363
  88.2 3.1 %collective-permute-done.20.refs_2_ = bf16[96,1024]{1,0:T(8,128)(2,1)S(1)} collective-permute-done((bf16[96,1024]{1,0:T(8,128)(2,1)S(1)}, bf16[96,1024]{1,0:T(8,128)(2,1)S(1)}, u32[]{:S(2)}, u32[]{:S(2)}) %collective-permute-start.20) | collective-permute-done | bytes 196640 | tf_op jit(solution)/shard_map/ppermute | solution.py:363
  94.5 10.8 %collective-permute-done.23.refs_5_ = bf16[96,1024]{1,0:T(8,128)(2,1)S(1)} collective-permute-done((bf16[96,1024]{1,0:T(8,128)(2,1)S(1)}, bf16[96,1024]{1,0:T(8,128)(2,1)S(1)}, u32[]{:S(2)}, u32[]{:S(2)}) %collective-permute-start.23) | collective-permute-done | bytes 196640 | tf_op jit(solution)/shard_map/ppermute | solution.py:363
  106.0 3.5 %shard_map.95.refs_8_ = bf16[32,32,768]{2,1,0:T(8,128)(2,1)} custom-call(bf16[96,1024]{1,0:T(8,128)(2,1)} %get-tuple-element.56.refs_0_, bf16[96,1024]{1,0:T(8,128)(2,1)} %copy-done.8, bf16[96,1024]{1,0:T(8,128)(2,1)} %copy-done.10, bf16[96,1024]{1,0:T(8,128)(2,1)} %copy-done.12, bf16[96,1024]{1,0:T(8,128)(2,1)} %copy-done.4, bf16[96,1024]{1,0:T(8,128)(2,1)} %copy-done.14, ...), custom_call_target="tpu_custom_call" | custom-call | bytes 3145728 | tf_op jit(solution)/shard_map/pallas_call | solution.py:258
  113.7 3.4 %collective-permute-done.10.refs_1_ = bf16[96,1024]{1,0:T(8,128)(2,1)S(1)} collective-permute-done((bf16[96,1024]{1,0:T(8,128)(2,1)}, bf16[96,1024]{1,0:T(8,128)(2,1)S(1)}, u32[]{:S(2)}, u32[]{:S(2)}) %collective-permute-start.10) | collective-permute-done | bytes 196640 | tf_op jit(solution)/shard_map/ppermute | solution.py:363
  122.9 3.6 %collective-permute-done.12.refs_3_ = bf16[96,1024]{1,0:T(8,128)(2,1)S(1)} collective-permute-done((bf16[96,1024]{1,0:T(8,128)(2,1)}, bf16[96,1024]{1,0:T(8,128)(2,1)S(1)}, u32[]{:S(2)}, u32[]{:S(2)}) %collective-permute-start.12) | collective-permute-done | bytes 196640 | tf_op jit(solution)/shard_map/ppermute | solution.py:363
  126.5 12.9 %collective-permute-done.14.refs_5_ = bf16[96,1024]{1,0:T(8,128)(2,1)S(1)} collective-permute-done((bf16[96,1024]{1,0:T(8,128)(2,1)}, bf16[96,1024]{1,0:T(8,128)(2,1)S(1)}, u32[]{:S(2)}, u32[]{:S(2)}) %collective-permute-start.14) | collective-permute-done | bytes 196640 | tf_op jit(solution)/shard_map/ppermute | solution.py:363
  140.7 3.5 %collective-permute-start.2 = (bf16[96,4096]{1,0:T(8,128)(2,1)S(1)}, bf16[96,4096]{1,0:T(8,128)(2,1)}, u32[]{:S(2)}, u32[]{:S(2)}) collective-permute-start(bf16[96,4096]{1,0:T(8,128)(2,1)S(1)} %collective-permute-done.1.refs_2_), channel_id=1, source_target_pairs={{0,2},{1,3},{2,0},{3,1},{4,6},{5,7},{6,4},{7,5},{8,10},{9,11},{10,... | collective-permute-start | bytes 2359304 | tf_op jit(solution)/shard_map/ppermute | solution.py:363
  144.3 6.9 %collective-permute-done.13.refs_4_ = bf16[96,1024]{1,0:T(8,128)(2,1)S(1)} collective-permute-done((bf16[96,1024]{1,0:T(8,128)(2,1)S(1)}, bf16[96,1024]{1,0:T(8,128)(2,1)S(1)}, u32[]{:S(2)}, u32[]{:S(2)}) %collective-permute-start.13) | collective-permute-done | bytes 196640 | tf_op jit(solution)/shard_map/ppermute | solution.py:363
  153.4 3.5 %shard_map.93.refs_8_ = bf16[32,32,768]{2,1,0:T(8,128)(2,1)} custom-call(bf16[96,1024]{1,0:T(8,128)(2,1)} %get-tuple-element.39.refs_0_, bf16[96,1024]{1,0:T(8,128)(2,1)} %copy-done.2, bf16[96,1024]{1,0:T(8,128)(2,1)} %copy-done.3, bf16[96,1024]{1,0:T(8,128)(2,1)} %copy-done.5, bf16[96,1024]{1,0:T(8,128)(2,1)} %copy-done.11, bf16[96,1024]{1,0:T(8,128)(2,1)} %copy-done.7, ...), custom_call_target="tpu_custom_call" | custom-call | bytes 3145728 | tf_op jit(solution)/shard_map/pallas_call | solution.py:258
  156.9 5.8 %collective-permute-done.2.refs_3_ = bf16[96,4096]{1,0:T(8,128)(2,1)} collective-permute-done((bf16[96,4096]{1,0:T(8,128)(2,1)S(1)}, bf16[96,4096]{1,0:T(8,128)(2,1)}, u32[]{:S(2)}, u32[]{:S(2)}) %collective-permute-start.2) | collective-permute-done | bytes 786464 | tf_op jit(solution)/shard_map/ppermute | solution.py:363
  162.8 16.8 %collective-permute-done.6.refs_5_ = bf16[96,4096]{1,0:T(8,128)(2,1)} collective-permute-done((bf16[96,4096]{1,0:T(8,128)(2,1)S(1)}, bf16[96,4096]{1,0:T(8,128)(2,1)}, u32[]{:S(2)}, u32[]{:S(2)}) %collective-permute-start.6) | collective-permute-done | bytes 786464 | tf_op jit(solution)/shard_map/ppermute | solution.py:363
  179.6 14.1 %collective-permute-done.8.refs_7_ = bf16[96,4096]{1,0:T(8,128)(2,1)} collective-permute-done((bf16[96,4096]{1,0:T(8,128)(2,1)S(1)}, bf16[96,4096]{1,0:T(8,128)(2,1)}, u32[]{:S(2)}, u32[]{:S(2)}) %collective-permute-start.8) | collective-permute-done | bytes 786464 | tf_op jit(solution)/shard_map/ppermute | solution.py:363
  193.7 23.6 %shard_map.96 = (f32[512,256]{1,0:T(8,128)}, f32[512,256]{1,0:T(8,128)}) custom-call(bf16[96,4096]{1,0:T(8,128)(2,1)} %shard_map.91.refs_0_, bf16[96,4096]{1,0:T(8,128)(2,1)} %collective-permute-done.refs_1_, bf16[96,4096]{1,0:T(8,128)(2,1)} %copy-done.20, bf16[96,4096]{1,0:T(8,128)(2,1)} %collective-permute-done.2.refs_3_, bf16[96,4096]{1,0:T(8,128)(2,1)} %copy-done, ...), custom_call_target="tpu_custom_call" | custom-call | flops 17179869184 | bytes 10485760 | tf_op jit(solution)/shard_map/pallas_call | solution.py:338
  218.5 24.0 %shard_map.97 = (f32[512,256]{1,0:T(8,128)}, f32[512,256]{1,0:T(8,128)}) custom-call(bf16[96,4096]{1,0:T(8,128)(2,1)} %shard_map.91.refs_0_, bf16[96,4096]{1,0:T(8,128)(2,1)} %collective-permute-done.refs_1_, bf16[96,4096]{1,0:T(8,128)(2,1)} %copy-done.20, bf16[96,4096]{1,0:T(8,128)(2,1)} %collective-permute-done.2.refs_3_, bf16[96,4096]{1,0:T(8,128)(2,1)} %copy-done, ...), custom_call_target="tpu_custom_call" | custom-call | flops 17179869184 | bytes 10485760 | tf_op jit(solution)/shard_map/pallas_call | solution.py:338
  246.8 6.5 %all-to-all-start = ((f32[16,32,256]{2,1,0:T(8,128)}), f32[16,32,256]{2,1,0:T(8,128)S(1)}, u32[]{:S(2)}, u32[]{:S(2)}) async-start(f32[16,32,256]{2,1,0:T(8,128)} %copy.20), calls=%async_computation | async-start | bytes 1048576 | tf_op jit(solution)/shard_map/all_to_all | solution.py:440
  253.5 15.1 %all-to-all-done = f32[16,32,256]{2,1,0:T(8,128)S(1)} async-done(((f32[16,32,256]{2,1,0:T(8,128)}), f32[16,32,256]{2,1,0:T(8,128)S(1)}, u32[]{:S(2)}, u32[]{:S(2)}) %all-to-all-start) | async-done | bytes 524320 | tf_op jit(solution)/shard_map/all_to_all | solution.py:440
  (109 shorter events, 36.8 us)
Async XLA Ops:
  6.8 20.8 %collective-permute-start.1 = (bf16[96,4096]{1,0:T(8,128)(2,1)}, bf16[96,4096]{1,0:T(8,128)(2,1)S(1)}, u32[]{:S(2)}, u32[]{:S(2)}) collective-permute-start(bf16[96,4096]{1,0:T(8,128)(2,1)} %shard_map.91.refs_0_), channel_id=1, source_target_pairs={{0,4},{1,5},{2,6},{3,7},{4,0},{5,1},{6,2},{7,3},{8,12},{9,13},{10,... | collective-permute-start | bytes 2359304 | tf_op jit(solution)/shard_map/ppermute | solution.py:363
  9.8 18.5 %collective-permute-start.4 = (bf16[96,4096]{1,0:T(8,128)(2,1)}, bf16[96,4096]{1,0:T(8,128)(2,1)S(1)}, u32[]{:S(2)}, u32[]{:S(2)}) collective-permute-start(bf16[96,4096]{1,0:T(8,128)(2,1)} %shard_map.91.refs_0_), channel_id=1, source_target_pairs={{4,8},{5,9},{6,10},{7,11},{8,4},{9,5},{10,6},{11,7},{20,24},{21,25... | collective-permute-start | bytes 2359304 | tf_op jit(solution)/shard_map/ppermute | solution.py:381
  27.6 23.4 %collective-permute-start.3 = (bf16[96,4096]{1,0:T(8,128)(2,1)S(1)}, bf16[96,4096]{1,0:T(8,128)(2,1)S(1)}, u32[]{:S(2)}, u32[]{:S(2)}) collective-permute-start(bf16[96,4096]{1,0:T(8,128)(2,1)S(1)} %collective-permute-done.1.refs_2_), channel_id=1, source_target_pairs={{4,8},{5,9},{6,10},{7,11},{8,4},{9,5},{10,6},{11,7},{20,24},{21,25... | collective-permute-start | bytes 2359304 | tf_op jit(solution)/shard_map/ppermute | solution.py:382
  28.3 24.3 %collective-permute-start.5 = (bf16[96,4096]{1,0:T(8,128)(2,1)S(1)}, bf16[96,4096]{1,0:T(8,128)(2,1)S(1)}, u32[]{:S(2)}, u32[]{:S(2)}) collective-permute-start(bf16[96,4096]{1,0:T(8,128)(2,1)S(1)} %collective-permute-done.4), channel_id=1, source_target_pairs={{4,0},{5,1},{6,2},{7,3},{8,12},{9,13},{10,14},{11,15},{20,16},{21,... | collective-permute-start | bytes 2359304 | tf_op jit(solution)/shard_map/ppermute | solution.py:383
  29.6 83.0 %collective-permute-start = (bf16[96,4096]{1,0:T(8,128)(2,1)}, bf16[96,4096]{1,0:T(8,128)(2,1)}, u32[]{:S(2)}, u32[]{:S(2)}) collective-permute-start(bf16[96,4096]{1,0:T(8,128)(2,1)} %shard_map.91.refs_0_), channel_id=1, source_target_pairs={{0,2},{1,3},{2,0},{3,1},{4,6},{5,7},{6,4},{7,5},{8,10},{9,11},{10,... | collective-permute-start | bytes 2359304 | tf_op jit(solution)/shard_map/ppermute | solution.py:363
  37.6 179.8 %collective-permute-start.18 = (bf16[32,256,256]{2,1,0:T(8,128)(2,1)}, bf16[32,256,256]{2,1,0:T(8,128)(2,1)}, u32[]{:S(2)}, u32[]{:S(2)}) collective-permute-start(bf16[32,256,256]{2,1,0:T(8,128)(2,1)} %shard_map.94.refs_10_), channel_id=1, source_target_pairs={{0,1},{1,0},{2,3},{3,2},{4,5},{5,4},{6,7},{7,6},{8,9},{9,8},{10,11... | collective-permute-start | bytes 12582920 | tf_op jit(solution)/shard_map/ppermute | solution.py:363
  50.9 30.1 %collective-permute-start.7 = (bf16[96,4096]{1,0:T(8,128)(2,1)S(1)}, bf16[96,4096]{1,0:T(8,128)(2,1)S(1)}, u32[]{:S(2)}, u32[]{:S(2)}) collective-permute-start(bf16[96,4096]{1,0:T(8,128)(2,1)S(1)} %collective-permute-done.3), channel_id=1, source_target_pairs={{4,0},{5,1},{6,2},{7,3},{8,12},{9,13},{10,14},{11,15},{20,16},{21,... | collective-permute-start | bytes 2359304 | tf_op jit(solution)/shard_map/ppermute | solution.py:384
  52.7 29.0 %collective-permute-start.22 = (bf16[96,1024]{1,0:T(8,128)(2,1)}, bf16[96,1024]{1,0:T(8,128)(2,1)S(1)}, u32[]{:S(2)}, u32[]{:S(2)}) collective-permute-start(bf16[96,1024]{1,0:T(8,128)(2,1)} %get-tuple-element.64), channel_id=1, source_target_pairs={{0,8},{1,9},{2,10},{3,11},{4,12},{5,13},{6,14},{7,15},{8,0},{9,1},... | collective-permute-start | bytes 589832 | tf_op jit(solution)/shard_map/ppermute | solution.py:363
  57.9 23.9 %collective-permute-start.9 = (bf16[96,1024]{1,0:T(8,128)(2,1)}, bf16[96,1024]{1,0:T(8,128)(2,1)S(1)}, u32[]{:S(2)}, u32[]{:S(2)}) collective-permute-start(bf16[96,1024]{1,0:T(8,128)(2,1)} %get-tuple-element.42), channel_id=1, source_target_pairs={{0,12},{1,13},{2,14},{3,15},{4,8},{5,9},{6,10},{7,11},{8,4},{9,5},... | collective-permute-start | bytes 589832 | tf_op jit(solution)/shard_map/ppermute | solution.py:363
  81.8 12.6 %collective-permute-start.21 = (bf16[96,1024]{1,0:T(8,128)(2,1)S(1)}, bf16[96,1024]{1,0:T(8,128)(2,1)S(1)}, u32[]{:S(2)}, u32[]{:S(2)}) collective-permute-start(bf16[96,1024]{1,0:T(8,128)(2,1)S(1)} %copy-done.25), channel_id=1, source_target_pairs={{0,6},{1,7},{2,4},{3,5},{4,2},{5,3},{6,0},{7,1},{8,14},{9,15},{10,... | collective-permute-start | bytes 589832 | tf_op jit(solution)/shard_map/ppermute | solution.py:363
  88.2 17.0 %collective-permute-start.23 = (bf16[96,1024]{1,0:T(8,128)(2,1)S(1)}, bf16[96,1024]{1,0:T(8,128)(2,1)S(1)}, u32[]{:S(2)}, u32[]{:S(2)}) collective-permute-start(bf16[96,1024]{1,0:T(8,128)(2,1)S(1)} %copy-done.24), channel_id=1, source_target_pairs={{0,10},{1,11},{2,8},{3,9},{4,14},{5,15},{6,12},{7,13},{8,2},{9,3},... | collective-permute-start | bytes 589832 | tf_op jit(solution)/shard_map/ppermute | solution.py:363
  91.3 13.9 %collective-permute-start.24 = (bf16[96,1024]{1,0:T(8,128)(2,1)S(1)}, bf16[96,1024]{1,0:T(8,128)(2,1)S(1)}, u32[]{:S(2)}, u32[]{:S(2)}) collective-permute-start(bf16[96,1024]{1,0:T(8,128)(2,1)S(1)} %copy-done.23), channel_id=1, source_target_pairs={{0,14},{1,15},{2,12},{3,13},{4,10},{5,11},{6,8},{7,9},{8,6},{9,7},... | collective-permute-start | bytes 589832 | tf_op jit(solution)/shard_map/ppermute | solution.py:363
  109.5 84.2 %collective-permute-start.25 = (bf16[32,32,768]{2,1,0:T(8,128)(2,1)}, bf16[32,32,768]{2,1,0:T(8,128)(2,1)}, u32[]{:S(2)}, u32[]{:S(2)}) collective-permute-start(bf16[32,32,768]{2,1,0:T(8,128)(2,1)} %shard_map.95.refs_8_), channel_id=1, source_target_pairs={{0,16},{16,0},{1,17},{17,1},{2,18},{18,2},{3,19},{19,3},{4,20},{20... | collective-permute-start | bytes 4718600 | tf_op jit(solution)/shard_map/ppermute | solution.py:427
  110.0 10.0 %collective-permute-start.11 = (bf16[96,1024]{1,0:T(8,128)(2,1)}, bf16[96,1024]{1,0:T(8,128)(2,1)S(1)}, u32[]{:S(2)}, u32[]{:S(2)}) collective-permute-start(bf16[96,1024]{1,0:T(8,128)(2,1)} %get-tuple-element.45), channel_id=1, source_target_pairs={{0,4},{1,5},{2,6},{3,7},{4,0},{5,1},{6,2},{7,3},{8,12},{9,13},{10,... | collective-permute-start | bytes 589832 | tf_op jit(solution)/shard_map/ppermute | solution.py:363
  112.5 14.0 %collective-permute-start.12 = (bf16[96,1024]{1,0:T(8,128)(2,1)}, bf16[96,1024]{1,0:T(8,128)(2,1)S(1)}, u32[]{:S(2)}, u32[]{:S(2)}) collective-permute-start(bf16[96,1024]{1,0:T(8,128)(2,1)} %get-tuple-element.47), channel_id=1, source_target_pairs={{0,6},{1,7},{2,4},{3,5},{4,2},{5,3},{6,0},{7,1},{8,14},{9,15},{10,... | collective-permute-start | bytes 589832 | tf_op jit(solution)/shard_map/ppermute | solution.py:363
  117.0 22.4 %collective-permute-start.14 = (bf16[96,1024]{1,0:T(8,128)(2,1)}, bf16[96,1024]{1,0:T(8,128)(2,1)S(1)}, u32[]{:S(2)}, u32[]{:S(2)}) collective-permute-start(bf16[96,1024]{1,0:T(8,128)(2,1)} %get-tuple-element.51), channel_id=1, source_target_pairs={{0,10},{1,11},{2,8},{3,9},{4,14},{5,15},{6,12},{7,13},{8,2},{9,3},... | collective-permute-start | bytes 589832 | tf_op jit(solution)/shard_map/ppermute | solution.py:363
  119.9 20.8 %collective-permute-start.16 = (bf16[96,1024]{1,0:T(8,128)(2,1)}, bf16[96,1024]{1,0:T(8,128)(2,1)S(1)}, u32[]{:S(2)}, u32[]{:S(2)}) collective-permute-start(bf16[96,1024]{1,0:T(8,128)(2,1)} %get-tuple-element.55), channel_id=1, source_target_pairs={{0,14},{1,15},{2,12},{3,13},{4,10},{5,11},{6,8},{7,9},{8,6},{9,7},... | collective-permute-start | bytes 589832 | tf_op jit(solution)/shard_map/ppermute | solution.py:363
  126.5 24.6 %collective-permute-start.13 = (bf16[96,1024]{1,0:T(8,128)(2,1)S(1)}, bf16[96,1024]{1,0:T(8,128)(2,1)S(1)}, u32[]{:S(2)}, u32[]{:S(2)}) collective-permute-start(bf16[96,1024]{1,0:T(8,128)(2,1)S(1)} %copy-done.22), channel_id=1, source_target_pairs={{0,8},{1,9},{2,10},{3,11},{4,12},{5,13},{6,14},{7,15},{8,0},{9,1},... | collective-permute-start | bytes 589832 | tf_op jit(solution)/shard_map/ppermute | solution.py:363
  139.5 13.2 %collective-permute-start.15 = (bf16[96,1024]{1,0:T(8,128)(2,1)S(1)}, bf16[96,1024]{1,0:T(8,128)(2,1)S(1)}, u32[]{:S(2)}, u32[]{:S(2)}) collective-permute-start(bf16[96,1024]{1,0:T(8,128)(2,1)S(1)} %copy-done.21), channel_id=1, source_target_pairs={{0,12},{1,13},{2,14},{3,15},{4,8},{5,9},{6,10},{7,11},{8,4},{9,5},... | collective-permute-start | bytes 589832 | tf_op jit(solution)/shard_map/ppermute | solution.py:363
  140.7 22.0 %collective-permute-start.2 = (bf16[96,4096]{1,0:T(8,128)(2,1)S(1)}, bf16[96,4096]{1,0:T(8,128)(2,1)}, u32[]{:S(2)}, u32[]{:S(2)}) collective-permute-start(bf16[96,4096]{1,0:T(8,128)(2,1)S(1)} %collective-permute-done.1.refs_2_), channel_id=1, source_target_pairs={{0,2},{1,3},{2,0},{3,1},{4,6},{5,7},{6,4},{7,5},{8,10},{9,11},{10,... | collective-permute-start | bytes 2359304 | tf_op jit(solution)/shard_map/ppermute | solution.py:363
  151.2 28.5 %collective-permute-start.6 = (bf16[96,4096]{1,0:T(8,128)(2,1)S(1)}, bf16[96,4096]{1,0:T(8,128)(2,1)}, u32[]{:S(2)}, u32[]{:S(2)}) collective-permute-start(bf16[96,4096]{1,0:T(8,128)(2,1)S(1)} %broadcast_select_fusion.1.refs_4_), channel_id=1, source_target_pairs={{0,2},{1,3},{2,0},{3,1},{4,6},{5,7},{6,4},{7,5},{8,10},{9,11},{10,... | collective-permute-start | bytes 2359304 | tf_op jit(solution)/shard_map/ppermute | solution.py:363
  152.7 41.0 %collective-permute-start.8 = (bf16[96,4096]{1,0:T(8,128)(2,1)S(1)}, bf16[96,4096]{1,0:T(8,128)(2,1)}, u32[]{:S(2)}, u32[]{:S(2)}) collective-permute-start(bf16[96,4096]{1,0:T(8,128)(2,1)S(1)} %broadcast_select_fusion.refs_6_), channel_id=1, source_target_pairs={{0,2},{1,3},{2,0},{3,1},{4,6},{5,7},{6,4},{7,5},{8,10},{9,11},{10,... | collective-permute-start | bytes 2359304 | tf_op jit(solution)/shard_map/ppermute | solution.py:363
  162.8 54.5 %collective-permute-start.17 = (bf16[32,32,768]{2,1,0:T(8,128)(2,1)}, bf16[32,32,768]{2,1,0:T(8,128)(2,1)S(1)}, u32[]{:S(2)}, u32[]{:S(2)}) collective-permute-start(bf16[32,32,768]{2,1,0:T(8,128)(2,1)} %shard_map.93.refs_8_), channel_id=1, source_target_pairs={{0,16},{16,0},{1,17},{17,1},{2,18},{18,2},{3,19},{19,3},{4,20},{20... | collective-permute-start | bytes 4718600 | tf_op jit(solution)/shard_map/ppermute | solution.py:427
  246.8 21.9 %all-to-all-start = ((f32[16,32,256]{2,1,0:T(8,128)}), f32[16,32,256]{2,1,0:T(8,128)S(1)}, u32[]{:S(2)}, u32[]{:S(2)}) async-start(f32[16,32,256]{2,1,0:T(8,128)} %copy.20), calls=%async_computation | async-start | bytes 1048576 | tf_op jit(solution)/shard_map/all_to_all | solution.py:440
  (32 other events, 892.3 us)
where the time goes:
time: 270 us; the launch traced here: 269 us
  waiting for transfers between devices  137 us (51%)
  Pallas kernels  79.5 us (29%)
  starting transfers between devices  46.2 us (17%)
  local copies, waits for them, and re-layouts  4.75 us (2%)
    ppermute x20, waiting for transfers between devices, exchange(): return lax.ppermute(value, 'dev', [(d, d ^ bits) for d in range(size)])  99.3 us
    pallas_call x2, Pallas kernels, ladder(): pl.pallas_call(functools.partial(ladder_kernel, slots, chunks, bool(start...  47.6 us
    ppermute x20, starting transfers between devices, exchange(): return lax.ppermute(value, 'dev', [(d, d ^ bits) for d in range(size)])  35.4 us
    ppermute x1, waiting for transfers between devices, plane_gather(): out_near = lax.ppermute(mid_near, 'dev', outward)  21.5 us
    all_to_all x1, waiting for transfers between devices, fast_body(): moved = lax.all_to_all(both, 'dev', split_axis=0, concat_axis=0, tiled=True)  15.1 us
    pallas_call x1, Pallas kernels, dress_b(): pl.pallas_call(functools.partial(dress_b_kernel, slots), out_shape=[out]...  11.8 us
    pallas_call x2, Pallas kernels, turn(): pl.pallas_call(functools.partial(turn_kernel, slots, d_tile), out_shape=j...  7.08 us
    pallas_call x1, Pallas kernels, dress_a(): pl.pallas_call(dress_a_kernel, out_shape=jax.ShapeDtypeStruct((shard, col...  6.77 us
  transfers between devices with their start and end apart: 28, of which 15 were waited for; matrix products, arithmetic and copies ran while one was open for 1% of the time, Pallas kernels for 18%

commit v1 on v0

--- a/solution.py
+++ b/solution.py
@@ -93,7 +93,7 @@
     )(doubles)
 
 
-def dress_a_kernel(where, f_ref, occ_ref, singles_ref, out, mix, order):
+def dress_a_kernel(where, f_ref, occ_ref, singles_ref, first, second, mix, order):
     a_rows = f_ref.shape[0] // TALL
     width = f_ref.shape[1]
 
@@ -103,17 +103,20 @@
         order[...] = reorder(TALL, a_rows, where[0] * (a_rows // 2))
 
     value = dressed(f_ref[...], occ_ref[...], mix, order).astype(BF16)
-    for a in range(a_rows):
-        out[:, a * width : (a + 1) * width] = value[a * TALL : (a + 1) * TALL]
+    half = a_rows // 2
+    for a in range(half):
+        at = slice(a * width, (a + 1) * width)
+        first[:, at] = value[a * TALL : (a + 1) * TALL]
+        second[:, at] = value[(half + a) * TALL : (half + a + 1) * TALL]
 
 
 def dress_a(col, factor_a, factor_occ, singles_a, c_tile):
     shard, a_rows, wide = factor_a.shape
     occ_rows = factor_occ.shape[1]
-    columns = a_rows * c_tile
+    columns = a_rows // 2 * c_tile
     return pl.pallas_call(
         dress_a_kernel,
-        out_shape=jax.ShapeDtypeStruct((shard, columns), BF16),
+        out_shape=[jax.ShapeDtypeStruct((shard, columns), BF16)] * 2,
         grid_spec=pltpu.PrefetchScalarGridSpec(
             num_scalar_prefetch=1,
             grid=(shard // TALL,),
@@ -122,7 +125,7 @@
                 pl.BlockSpec((TALL * occ_rows, c_tile), lambda i, w: (i, w[0])),
                 pl.BlockSpec(singles_a.shape, lambda i, w: (0, 0)),
             ],
-            out_specs=pl.BlockSpec((TALL, columns), lambda i, w: (i, 0)),
+            out_specs=[pl.BlockSpec((TALL, columns), lambda i, w: (i, 0))] * 2,
             scratch_shapes=[
                 pltpu.VMEM((TALL * a_rows, 3 * TALL * occ_rows), BF16),
                 pltpu.VMEM((TALL * a_rows, TALL * a_rows), BF16),
@@ -269,12 +272,12 @@
     )(*blocks)
 
 
-def ladder_kernel(slots, chunks, has_start, *refs):
+def ladder_kernel(slots, chunks, has_start, own_rows, *refs):
     n = slots * chunks
     a_refs, (own_ref, other_ref, t_ref) = refs[:n], refs[n : n + 3]
     refs = refs[n + 3 :]
-    starts, refs = (refs[:2], refs[2:]) if has_start else ((), refs)
-    keep_ref, send_ref, whole_a, integral, total, sems = refs
+    starts, refs = (refs[:chunks], refs[chunks:]) if has_start else ((), refs)
+    outs, (whole_a, integral, total, sems) = refs[:chunks], refs[chunks:]
     step = pl.program_id(0)
     shard, width = a_refs[0].shape
 
@@ -289,15 +292,15 @@
             for k in range(slots)
         ]
 
-    half = total.shape[0] // 2
+    part = total.shape[0] // chunks
 
     @pl.when(step == 0)
     def _():
         for copy in copies():
             copy.start()
         if has_start:
-            total[:half, :] = starts[0][...]
-            total[half:, :] = starts[1][...]
+            for n in range(chunks):
+                total[n * part : (n + 1) * part, :] = starts[n][...]
         else:
             total[...] = jnp.zeros_like(total)
         for copy in copies():
@@ -321,11 +324,20 @@
 
     @pl.when(step == pl.num_programs(0) - 1)
     def _():
-        keep_ref[...] = total[:half, :]
-        send_ref[...] = total[half:, :]
-
-
-def ladder(a_blocks, own, other, doubles, starts, d_rows=8):
+        for n, out in enumerate(outs):
+            if own_rows is None:
+                out[...] = total[n * part : (n + 1) * part, :]
+                continue
+            for a in range(part // b_all):
+                for b in range(0, b_all, own_rows):
+                    source = n * part + a * b_all + b
+                    side, owner = divmod(b, b_local)
+                    out[side, owner // own_rows, a * own_rows : (a + 1) * own_rows, :] = total[
+                        source : source + own_rows, :
+                    ]
+
+
+def ladder(a_blocks, own, other, doubles, starts, own_rows=None, d_rows=8):
     chunks, slots = len(a_blocks), len(a_blocks[0])
     _, width = a_blocks[0][0].shape
     d_tile, b_local, depth = own.shape
@@ -333,17 +345,21 @@
     columns = chunks * width
     a_rows = columns // c_tile
     rows = a_rows * 2 * b_local
-    out = jax.ShapeDtypeStruct((rows // 2, pairs), F32)
-    full = pl.BlockSpec((rows // 2, pairs), lambda i: (0, 0))
+    full = pl.BlockSpec((rows // chunks, pairs), lambda i: (0, 0))
+    if own_rows is None:
+        out, out_spec = jax.ShapeDtypeStruct((rows // chunks, pairs), F32), full
+    else:
+        shape = (2, b_local // own_rows, a_rows // chunks * own_rows, pairs)
+        out, out_spec = jax.ShapeDtypeStruct(shape, F32), pl.BlockSpec(shape, lambda i: (0,) * 4)
     return pl.pallas_call(
-        functools.partial(ladder_kernel, slots, chunks, bool(starts)),
-        out_shape=[out, out],
+        functools.partial(ladder_kernel, slots, chunks, bool(starts), own_rows),
+        out_shape=[out] * chunks,
         grid=(d_tile // d_rows,),
         in_specs=[pl.BlockSpec(memory_space=pl.ANY)] * (chunks * slots)
         + [pl.BlockSpec((d_rows, b_local, depth), lambda i: (i, 0, 0))] * 2
         + [pl.BlockSpec((d_rows, c_tile, pairs), lambda i: (i, 0, 0))]
         + [full] * len(starts),
-        out_specs=[full, full],
+        out_specs=[out_spec] * chunks,
         scratch_shapes=[
             pltpu.VMEM((depth, columns), BF16),
             pltpu.VMEM((rows, d_rows * c_tile), BF16),
@@ -387,7 +403,7 @@
     found = []
     for part in (block, near, far, farthest):
         found += [part, exchange(part, link, size)]
-    return found, (near, mid_near, out_own, far, farthest)
+    return found, dict(near=near, far=far, farthest=farthest)
 
 
 def fast_body(
@@ -405,40 +421,35 @@
     c_tile, d_tile, pairs = doubles.shape
     a_rows, b_local = factor_a.shape[1], factor_b.shape[1]
     slots = size // 2
+    b_own = 2 * b_local // size
     col = lax.axis_index("col").astype(jnp.int32)
     dev = lax.axis_index("dev").astype(jnp.int32)
-    block_a = dress_a(col, factor_a, factor_occ, singles_a, c_tile)
+    blocks_a = dress_a(col, factor_a, factor_occ, singles_a, c_tile)
     mine = swap_doubles(doubles)
     theirs = exchange(mine, 1, size)
-    whole_a, (near, mid_near, out_own, far, farthest) = plane_gather(block_a, size, 2)
+    whole0, marks0 = plane_gather(blocks_a[0], size, 2)
+    whole1, marks1 = plane_gather(gated(blocks_a[1], marks0["near"]), size, 2)
     halves = dress_b(dev, factor_b, factor_occ, singles_b, d_tile, slots)
-    partial_value = ()
-    order = [slot for slot in (4, 6, 5, 7, 2, 3, 1) if slot < slots]
-    for n, (half, weights) in enumerate(zip(halves, (mine, theirs))):
+    order = [slot for slot in (4, 6, 2, 5, 7, 3, 1) if slot < slots]
+    sides = []
+    for n, half in enumerate(halves):
         found = {0: half[0]}
         for slot in order:
-            if n:
-                gate = farthest if slot in order[:2] else first[order[1]]
-            else:
-                gate = far if slot in order[:2] else farthest
+            gate = marks1["farthest"] if n else marks0["far"]
             found[slot] = exchange(gated(half[slot], gate), 2 * slot, size)
-        first = found
         own = turn([found[k] for k in range(slots)], d_tile)
         other = lax.ppermute(own, "col", [(0, 1), (1, 0)])
-        partial_value = ladder([whole_a], own, other, weights, tuple(partial_value))
-    keep, send = partial_value
+        sides.append((own, other))
+    (keep,) = ladder([whole0], *sides[0], mine, (), d_rows=4)
+    (send,) = ladder([whole1], *sides[0], mine, (), d_rows=4)
+    keep, send = ladder([whole0, whole1], *sides[1], theirs, (keep, send), b_own)
     got = lax.ppermute(send, "col", [(0, 1), (1, 0)])
+    near, far = keep[0] + got[1], keep[1] + got[0]
+    both = jnp.where(col == 0, jnp.stack([near, far]), jnp.stack([far, near]))
     a_half = a_rows // 2
-    keep = keep.reshape(a_half, 2, b_local, pairs)
-    got = got.reshape(a_half, 2, b_local, pairs)
-    first = jnp.where(col == 0, keep[:, 0] + got[:, 1], keep[:, 1] + got[:, 0])
-    second = jnp.where(col == 0, keep[:, 1] + got[:, 0], keep[:, 0] + got[:, 1])
-    both = jnp.stack([first, second])
-    b_own = 2 * b_local // size
-    both = both.reshape(2, a_half, size // 2, b_own, pairs)
-    both = jnp.transpose(both, (0, 2, 1, 3, 4)).reshape(size, a_half * b_own, pairs)
+    both = both.astype(BF16).reshape(size, a_half * b_own, pairs)
     moved = lax.all_to_all(both, "dev", split_axis=0, concat_axis=0, tiled=True)
-    total = jnp.sum(moved, axis=0).reshape(a_half, b_own, pairs)
+    total = jnp.sum(moved.astype(F32), axis=0).reshape(a_half, b_own, pairs)
     pair_energy = (orbital_occ[:, None] + orbital_occ[None, :]).reshape(-1)
     denominator = orbital_a[:, None, None] + orbital_b[None, :, None] - pair_energy[None, None, :]
     return total / denominator

time: 270 us -> 268 us (level)
  waiting for transfers between devices: 137 us -> 122 us
  starting transfers between devices: 46.2 us -> 55.1 us
  Pallas kernels: 79.5 us -> 84.9 us
  local copies, waits for them, and re-layouts: 4.75 us -> 1.37 us
    ppermute x1 -> x2, waiting for transfers between devices: 0.01 us -> 21.5 us  [plane_gather(): out_own = lax.ppermute(mid_own, 'dev', outward)]
    ppermute x1 -> x2, waiting for transfers between devices: 21.5 us -> 0.01 us  [plane_gather(): out_near = lax.ppermute(mid_near, 'dev', outward)]
    ppermute x20 -> x25, waiting for transfers between devices: 99.3 us -> 88.5 us  [exchange(): return lax.ppermute(value, 'dev', [(d, d ^ bits) for d in range(size)])]
    ppermute x20 -> x25, starting transfers between devices: 35.4 us -> 41.3 us  [exchange(): return lax.ppermute(value, 'dev', [(d, d ^ bits) for d in range(size)])]
    all_to_all x1, waiting for transfers between devices: 15.1 us -> 9.93 us  [fast_body(): moved = lax.all_to_all(both, 'dev', split_axis=0, concat_axis=0, tiled=True)]
    pallas_call x2 -> x3, Pallas kernels: 47.6 us -> 52.8 us  [ladder(): pl.pallas_call(functools.partial(ladder_kernel, slots, chunks, bool(start...]
  transfers between devices with their start and end apart: 28 -> 37, of which waited for: 15 -> 20; matrix products, arithmetic and copies ran while one was open for 1% -> 0% of each run, Pallas kernels for 18% -> 20%
where the time goes in v1:
time: 268 us; the launch traced here: 267 us
  waiting for transfers between devices  122 us (46%)
  Pallas kernels  84.9 us (32%)
  starting transfers between devices  55.1 us (21%)
  other arithmetic  2.91 us (1%)
    ppermute x25, waiting for transfers between devices, exchange(): return lax.ppermute(value, 'dev', [(d, d ^ bits) for d in range(size)])  88.5 us
    pallas_call x3, Pallas kernels, ladder(): pl.pallas_call(functools.partial(ladder_kernel, slots, chunks, bool(start...  52.8 us
    ppermute x25, starting transfers between devices, exchange(): return lax.ppermute(value, 'dev', [(d, d ^ bits) for d in range(size)])  41.3 us
    ppermute x2, waiting for transfers between devices, plane_gather(): out_own = lax.ppermute(mid_own, 'dev', outward)  21.5 us
    pallas_call x1, Pallas kernels, dress_b(): pl.pallas_call(functools.partial(dress_b_kernel, slots), out_shape=[out]...  11.9 us
    all_to_all x1, waiting for transfers between devices, fast_body(): moved = lax.all_to_all(both, 'dev', split_axis=0, concat_axis=0, tiled=True)  9.93 us
    pallas_call x2, Pallas kernels, turn(): pl.pallas_call(functools.partial(turn_kernel, slots, d_tile), out_shape=j...  7.15 us
    pallas_call x1, Pallas kernels, dress_a(): pl.pallas_call(dress_a_kernel, out_shape=[jax.ShapeDtypeStruct((shard, co...  6.71 us
  transfers between devices with their start and end apart: 37, of which 20 were waited for; matrix products, arithmetic and copies ran while one was open for 0% of the time, Pallas kernels for 20%

profile of v1, /device:TPU:0, one launch (start us, length us, event | category | flops | bytes accessed | tf_op | source)
XLA Modules:
  0.0 266.8 jit_solution(7138649775553372308)
XLA Ops:
  0.0 6.7 %shard_map.91 = (bf16[96,2048]{1,0:T(8,128)(2,1)}, bf16[96,2048]{1,0:T(8,128)(2,1)}) custom-call(s32[1]{0:T(128)} %bitcast.where, f32[1536,512]{1,0:T(8,128)} %bitcast.15, f32[1536,512]{1,0:T(8,128)} %bitcast.10, f32[16,16]{1,0:T(8,128)} %singles_ref.1), custom_call_target="tpu_custom_call" | custom-call | flops 12582912 | bytes 3932160 | tf_op jit(solution)/shard_map/pallas_call | solution.py:117
  10.4 8.6 %collective-permute-done.1.refs_2_ = bf16[96,2048]{1,0:T(8,128)(2,1)S(1)} collective-permute-done((bf16[96,2048]{1,0:T(8,128)(2,1)}, bf16[96,2048]{1,0:T(8,128)(2,1)S(1)}, u32[]{:S(2)}, u32[]{:S(2)}) %collective-permute-start.1) | collective-permute-done | bytes 393248 | tf_op jit(solution)/shard_map/ppermute | solution.py:379
  21.1 11.9 %shard_map.92 = (bf16[96,1024]{1,0:T(8,128)(2,1)}, bf16[96,1024]{1,0:T(8,128)(2,1)}, bf16[96,1024]{1,0:T(8,128)(2,1)}, bf16[96,1024]{1,0:T(8,128)(2,1)}, bf16[96...) custom-call(s32[1]{0:T(128)} %bitcast.3.where, ...), custom_call_target="tpu_custom_call" | custom-call | flops 50331648 | bytes 12582912 | tf_op jit(solution)/shard_map/pallas_call | solution.py:211
  33.0 4.6 %collective-permute-start.10 = (bf16[96,2048]{1,0:T(8,128)(2,1)}, bf16[96,2048]{1,0:T(8,128)(2,1)S(1)}, u32[]{:S(2)}, u32[]{:S(2)}) collective-permute-start(bf16[96,2048]{1,0:T(8,128)(2,1)} %get-tuple-element.42.refs_0_.refs_8_), channel_id=1, source_target_pairs={{0,4},{1,5},{2,6},{3,7},{4,0},{5,1},{6,2},{7,3},{8,12},{9,13},{10,... | collective-permute-start | bytes 1179656 | tf_op jit(solution)/shard_map/ppermute | solution.py:379
  39.4 8.4 %collective-permute-done.10.refs_2_.refs_10_ = bf16[96,2048]{1,0:T(8,128)(2,1)S(1)} collective-permute-done((bf16[96,2048]{1,0:T(8,128)(2,1)}, bf16[96,2048]{1,0:T(8,128)(2,1)S(1)}, u32[]{:S(2)}, u32[]{:S(2)}) %collective-permute-start.10) | collective-permute-done | bytes 393248 | tf_op jit(solution)/shard_map/ppermute | solution.py:379
  48.5 6.3 %shard_map.94.refs_10_ = bf16[32,256,256]{2,1,0:T(8,128)(2,1)} custom-call(bf16[256,32,256]{2,1,0:T(8,128)(2,1)} %t_ref.1), custom_call_target="tpu_custom_call" | custom-call | bytes 8388608 | tf_op jit(solution)/shard_map/pallas_call | solution.py:82
  56.3 5.3 %collective-permute-start.29 = (bf16[96,1024]{1,0:T(8,128)(2,1)S(1)}, bf16[96,1024]{1,0:T(8,128)(2,1)S(1)}, u32[]{:S(2)}, u32[]{:S(2)}) collective-permute-start(bf16[96,1024]{1,0:T(8,128)(2,1)S(1)} %copy-done.30), channel_id=1, source_target_pairs={{0,6},{1,7},{2,4},{3,5},{4,2},{5,3},{6,0},{7,1},{8,14},{9,15},{10,... | collective-permute-start | bytes 589832 | tf_op jit(solution)/shard_map/ppermute | solution.py:379
  68.6 10.1 %collective-permute-done.30.refs_4_ = bf16[96,1024]{1,0:T(8,128)(2,1)S(1)} collective-permute-done((bf16[96,1024]{1,0:T(8,128)(2,1)S(1)}, bf16[96,1024]{1,0:T(8,128)(2,1)S(1)}, u32[]{:S(2)}, u32[]{:S(2)}) %collective-permute-start.30) | collective-permute-done | bytes 196640 | tf_op jit(solution)/shard_map/ppermute | solution.py:379
  79.2 3.6 %collective-permute-done.31.refs_5_ = bf16[96,1024]{1,0:T(8,128)(2,1)S(1)} collective-permute-done((bf16[96,1024]{1,0:T(8,128)(2,1)S(1)}, bf16[96,1024]{1,0:T(8,128)(2,1)S(1)}, u32[]{:S(2)}, u32[]{:S(2)}) %collective-permute-start.31) | collective-permute-done | bytes 196640 | tf_op jit(solution)/shard_map/ppermute | solution.py:379
  87.8 5.7 %collective-permute-done.33.refs_7_ = bf16[96,1024]{1,0:T(8,128)(2,1)S(1)} collective-permute-done((bf16[96,1024]{1,0:T(8,128)(2,1)S(1)}, bf16[96,1024]{1,0:T(8,128)(2,1)S(1)}, u32[]{:S(2)}, u32[]{:S(2)}) %collective-permute-start.33) | collective-permute-done | bytes 196640 | tf_op jit(solution)/shard_map/ppermute | solution.py:379
  95.1 3.5 %shard_map.95.refs_8_ = bf16[32,32,768]{2,1,0:T(8,128)(2,1)} custom-call(bf16[96,1024]{1,0:T(8,128)(2,1)} %get-tuple-element.58.refs_0_, bf16[96,1024]{1,0:T(8,128)(2,1)} %copy-done.4, bf16[96,1024]{1,0:T(8,128)(2,1)} %copy-done.5, bf16[96,1024]{1,0:T(8,128)(2,1)} %copy-done.9, bf16[96,1024]{1,0:T(8,128)(2,1)} %copy-done.11, bf16[96,1024]{1,0:T(8,128)(2,1)} %copy-done.13, ...), custom_call_target="tpu_custom_call" | custom-call | bytes 3145728 | tf_op jit(solution)/shard_map/pallas_call | solution.py:261
  103.5 21.5 %collective-permute-done.14 = bf16[96,2048]{1,0:T(8,128)(2,1)S(1)} collective-permute-done((bf16[96,2048]{1,0:T(8,128)(2,1)S(1)}, bf16[96,2048]{1,0:T(8,128)(2,1)S(1)}, u32[]{:S(2)}, u32[]{:S(2)}) %collective-permute-start.14) | collective-permute-done | bytes 393248 | tf_op jit(solution)/shard_map/ppermute | solution.py:399
  127.4 8.3 %collective-permute-done.19.refs_2_ = bf16[96,1024]{1,0:T(8,128)(2,1)S(1)} collective-permute-done((bf16[96,1024]{1,0:T(8,128)(2,1)}, bf16[96,1024]{1,0:T(8,128)(2,1)S(1)}, u32[]{:S(2)}, u32[]{:S(2)}) %collective-permute-start.19) | collective-permute-done | bytes 196640 | tf_op jit(solution)/shard_map/ppermute | solution.py:379
  140.7 9.2 %collective-permute-done.21.refs_4_ = bf16[96,1024]{1,0:T(8,128)(2,1)S(1)} collective-permute-done((bf16[96,1024]{1,0:T(8,128)(2,1)}, bf16[96,1024]{1,0:T(8,128)(2,1)S(1)}, u32[]{:S(2)}, u32[]{:S(2)}) %collective-permute-start.21) | collective-permute-done | bytes 196640 | tf_op jit(solution)/shard_map/ppermute | solution.py:379
  160.0 3.6 %shard_map.93.refs_16_ = bf16[32,32,768]{2,1,0:T(8,128)(2,1)} custom-call(bf16[96,1024]{1,0:T(8,128)(2,1)} %get-tuple-element.43.refs_0_, bf16[96,1024]{1,0:T(8,128)(2,1)} %copy-done.6, bf16[96,1024]{1,0:T(8,128)(2,1)} %copy-done.7, bf16[96,1024]{1,0:T(8,128)(2,1)} %copy-done.8, bf16[96,1024]{1,0:T(8,128)(2,1)} %copy-done.10, bf16[96,1024]{1,0:T(8,128)(2,1)} %copy-done.12, ...), custom_call_target="tpu_custom_call" | custom-call | bytes 3145728 | tf_op jit(solution)/shard_map/pallas_call | solution.py:261
  163.6 3.6 %collective-permute-done.11.refs_3_.refs_11_ = bf16[96,2048]{1,0:T(8,128)(2,1)} collective-permute-done((bf16[96,2048]{1,0:T(8,128)(2,1)}, bf16[96,2048]{1,0:T(8,128)(2,1)}, u32[]{:S(2)}, u32[]{:S(2)}) %collective-permute-start.11) | collective-permute-done | bytes 393248 | tf_op jit(solution)/shard_map/ppermute | solution.py:379
  168.4 7.2 %collective-permute-done.15.refs_5_.refs_13_ = bf16[96,2048]{1,0:T(8,128)(2,1)} collective-permute-done((bf16[96,2048]{1,0:T(8,128)(2,1)S(1)}, bf16[96,2048]{1,0:T(8,128)(2,1)}, u32[]{:S(2)}, u32[]{:S(2)}) %collective-permute-start.15) | collective-permute-done | bytes 393248 | tf_op jit(solution)/shard_map/ppermute | solution.py:379
  176.8 7.2 %collective-permute-done.17.refs_7_.refs_15_ = bf16[96,2048]{1,0:T(8,128)(2,1)} collective-permute-done((bf16[96,2048]{1,0:T(8,128)(2,1)S(1)}, bf16[96,2048]{1,0:T(8,128)(2,1)}, u32[]{:S(2)}, u32[]{:S(2)}) %collective-permute-start.17) | collective-permute-done | bytes 393248 | tf_op jit(solution)/shard_map/ppermute | solution.py:379
  185.2 14.3 %shard_map.97.refs_20_ = f32[512,256]{1,0:T(8,128)} custom-call(bf16[96,2048]{1,0:T(8,128)(2,1)} %get-tuple-element.42.refs_0_.refs_8_, bf16[96,2048]{1,0:T(8,128)(2,1)} %collective-permute-done.9.refs_1_.refs_9_, bf16[96,2048]{1,0:T(8,128)(2,1)} %copy-done.24, bf16[96,2048]{1,0:T(8,128)(2,1)} %collective-permute-done.11.refs_3_.refs_11_, ...), custom_call_target="tpu_custom_call" | custom-call | flops 8589934592 | bytes 7340032 | tf_op jit(solution)/shard_map/pallas_call | solution.py:354
  200.9 5.8 %collective-permute-done.8.refs_7_ = bf16[96,2048]{1,0:T(8,128)(2,1)} collective-permute-done((bf16[96,2048]{1,0:T(8,128)(2,1)S(1)}, bf16[96,2048]{1,0:T(8,128)(2,1)}, u32[]{:S(2)}, u32[]{:S(2)}) %collective-permute-start.8) | collective-permute-done | bytes 393248 | tf_op jit(solution)/shard_map/ppermute | solution.py:379
  206.7 14.3 %shard_map.96.refs_19_ = f32[512,256]{1,0:T(8,128)} custom-call(bf16[96,2048]{1,0:T(8,128)(2,1)} %get-tuple-element.40.refs_0_, bf16[96,2048]{1,0:T(8,128)(2,1)} %collective-permute-done.refs_1_, bf16[96,2048]{1,0:T(8,128)(2,1)} %copy-done.22, bf16[96,2048]{1,0:T(8,128)(2,1)} %copy-done.25, bf16[96,2048]{1,0:T(8,128)(2,1)} %copy-done, ...), custom_call_target="tpu_custom_call" | custom-call | flops 8589934592 | bytes 7340032 | tf_op jit(solution)/shard_map/pallas_call | solution.py:354
  222.2 24.2 %shard_map.98 = (f32[2,8,32,256]{3,2,1,0:T(8,128)}, f32[2,8,32,256]{3,2,1,0:T(8,128)}) custom-call(bf16[96,2048]{1,0:T(8,128)(2,1)} %get-tuple-element.40.refs_0_, bf16[96,2048]{1,0:T(8,128)(2,1)} %collective-permute-done.refs_1_, bf16[96,2048]{1,0:T(8,128)(2,1)} %copy-done.22, bf16[96,2048]{1,0:T(8,128)(2,1)} %copy-done.25, bf16[96,2048]{1,0:T(8,128)(2,1)} %copy-done, ...), custom_call_target="tpu_custom_call" | custom-call | flops 17179869184 | bytes 10485760 | tf_op jit(solution)/shard_map/pallas_call | solution.py:354
  250.4 5.5 %all-to-all-start = ((bf16[16,32,256]{2,1,0:T(8,128)(2,1)}), bf16[16,32,256]{2,1,0:T(8,128)(2,1)S(1)}, u32[]{:S(2)}, u32[]{:S(2)}) async-start(bf16[16,32,256]{2,1,0:T(8,128)(2,1)} %bitcast.5), calls=%async_computation | async-start | bytes 524288 | tf_op jit(solution)/shard_map/all_to_all | solution.py:451
  256.1 9.9 %all-to-all-done = bf16[16,32,256]{2,1,0:T(8,128)(2,1)S(1)} async-done(((bf16[16,32,256]{2,1,0:T(8,128)(2,1)}), bf16[16,32,256]{2,1,0:T(8,128)(2,1)S(1)}, u32[]{:S(2)}, u32[]{:S(2)}) %all-to-all-start) | async-done | bytes 262176 | tf_op jit(solution)/shard_map/all_to_all | solution.py:451
  (132 shorter events, 56.7 us)
Async XLA Ops:
  19.1 18.6 %collective-permute-start.3 = (bf16[96,2048]{1,0:T(8,128)(2,1)S(1)}, bf16[96,2048]{1,0:T(8,128)(2,1)S(1)}, u32[]{:S(2)}, u32[]{:S(2)}) collective-permute-start(bf16[96,2048]{1,0:T(8,128)(2,1)S(1)} %collective-permute-done.1.refs_2_), channel_id=1, source_target_pairs={{4,8},{5,9},{6,10},{7,11},{8,4},{9,5},{10,6},{11,7},{20,24},{21,25... | collective-permute-start | bytes 1179656 | tf_op jit(solution)/shard_map/ppermute | solution.py:398
  19.8 17.9 %collective-permute-start.5 = (bf16[96,2048]{1,0:T(8,128)(2,1)S(1)}, bf16[96,2048]{1,0:T(8,128)(2,1)S(1)}, u32[]{:S(2)}, u32[]{:S(2)}) collective-permute-start(bf16[96,2048]{1,0:T(8,128)(2,1)S(1)} %collective-permute-done.4), channel_id=1, source_target_pairs={{4,0},{5,1},{6,2},{7,3},{8,12},{9,13},{10,14},{11,15},{20,16},{21,... | collective-permute-start | bytes 1179656 | tf_op jit(solution)/shard_map/ppermute | solution.py:399
  37.7 23.9 %collective-permute-start.27 = (bf16[96,1024]{1,0:T(8,128)(2,1)}, bf16[96,1024]{1,0:T(8,128)(2,1)S(1)}, u32[]{:S(2)}, u32[]{:S(2)}) collective-permute-start(bf16[96,1024]{1,0:T(8,128)(2,1)} %get-tuple-element.60), channel_id=1, source_target_pairs={{0,2},{1,3},{2,0},{3,1},{4,6},{5,7},{6,4},{7,5},{8,10},{9,11},{10,... | collective-permute-start | bytes 589832 | tf_op jit(solution)/shard_map/ppermute | solution.py:379
  39.3 22.3 %collective-permute-start.28 = (bf16[96,1024]{1,0:T(8,128)(2,1)}, bf16[96,1024]{1,0:T(8,128)(2,1)S(1)}, u32[]{:S(2)}, u32[]{:S(2)}) collective-permute-start(bf16[96,1024]{1,0:T(8,128)(2,1)} %get-tuple-element.62), channel_id=1, source_target_pairs={{0,4},{1,5},{2,6},{3,7},{4,0},{5,1},{6,2},{7,3},{8,12},{9,13},{10,... | collective-permute-start | bytes 589832 | tf_op jit(solution)/shard_map/ppermute | solution.py:379
  47.8 35.7 %collective-permute-start.12 = (bf16[96,2048]{1,0:T(8,128)(2,1)S(1)}, bf16[96,2048]{1,0:T(8,128)(2,1)S(1)}, u32[]{:S(2)}, u32[]{:S(2)}) collective-permute-start(bf16[96,2048]{1,0:T(8,128)(2,1)S(1)} %collective-permute-done.10.refs_2_.refs_10_), channel_id=1, source_target_pairs={{4,8},{5,9},{6,10},{7,11},{8,4},{9,5},{10,6},{11,7},{20,24},{21,25... | collective-permute-start | bytes 1179656 | tf_op jit(solution)/shard_map/ppermute | solution.py:398
  54.8 166.2 %collective-permute-start.26 = (bf16[32,256,256]{2,1,0:T(8,128)(2,1)}, bf16[32,256,256]{2,1,0:T(8,128)(2,1)}, u32[]{:S(2)}, u32[]{:S(2)}) collective-permute-start(bf16[32,256,256]{2,1,0:T(8,128)(2,1)} %shard_map.94.refs_10_), channel_id=1, source_target_pairs={{0,1},{1,0},{2,3},{3,2},{4,5},{5,4},{6,7},{7,6},{8,9},{9,8},{10,11... | collective-permute-start | bytes 12582920 | tf_op jit(solution)/shard_map/ppermute | solution.py:379
  61.6 17.1 %collective-permute-start.30 = (bf16[96,1024]{1,0:T(8,128)(2,1)S(1)}, bf16[96,1024]{1,0:T(8,128)(2,1)S(1)}, u32[]{:S(2)}, u32[]{:S(2)}) collective-permute-start(bf16[96,1024]{1,0:T(8,128)(2,1)S(1)} %copy-done.29), channel_id=1, source_target_pairs={{0,8},{1,9},{2,10},{3,11},{4,12},{5,13},{6,14},{7,15},{8,0},{9,1},... | collective-permute-start | bytes 589832 | tf_op jit(solution)/shard_map/ppermute | solution.py:379
  61.7 21.1 %collective-permute-start.31 = (bf16[96,1024]{1,0:T(8,128)(2,1)S(1)}, bf16[96,1024]{1,0:T(8,128)(2,1)S(1)}, u32[]{:S(2)}, u32[]{:S(2)}) collective-permute-start(bf16[96,1024]{1,0:T(8,128)(2,1)S(1)} %copy-done.28), channel_id=1, source_target_pairs={{0,10},{1,11},{2,8},{3,9},{4,14},{5,15},{6,12},{7,13},{8,2},{9,3},... | collective-permute-start | bytes 589832 | tf_op jit(solution)/shard_map/ppermute | solution.py:379
  66.9 18.0 %collective-permute-start.32 = (bf16[96,1024]{1,0:T(8,128)(2,1)S(1)}, bf16[96,1024]{1,0:T(8,128)(2,1)S(1)}, u32[]{:S(2)}, u32[]{:S(2)}) collective-permute-start(bf16[96,1024]{1,0:T(8,128)(2,1)S(1)} %copy-done.27), channel_id=1, source_target_pairs={{0,12},{1,13},{2,14},{3,15},{4,8},{5,9},{6,10},{7,11},{8,4},{9,5},... | collective-permute-start | bytes 589832 | tf_op jit(solution)/shard_map/ppermute | solution.py:379
  78.7 19.9 %collective-permute-start = (bf16[96,2048]{1,0:T(8,128)(2,1)}, bf16[96,2048]{1,0:T(8,128)(2,1)}, u32[]{:S(2)}, u32[]{:S(2)}) collective-permute-start(bf16[96,2048]{1,0:T(8,128)(2,1)} %get-tuple-element.40.refs_0_), channel_id=1, source_target_pairs={{0,2},{1,3},{2,0},{3,1},{4,6},{5,7},{6,4},{7,5},{8,10},{9,11},{10,... | collective-permute-start | bytes 1179656 | tf_op jit(solution)/shard_map/ppermute | solution.py:379
  82.8 17.2 %collective-permute-start.13 = (bf16[96,2048]{1,0:T(8,128)(2,1)}, bf16[96,2048]{1,0:T(8,128)(2,1)S(1)}, u32[]{:S(2)}, u32[]{:S(2)}) collective-permute-start(bf16[96,2048]{1,0:T(8,128)(2,1)} %get-tuple-element.42.refs_0_.refs_8_), channel_id=1, source_target_pairs={{4,8},{5,9},{6,10},{7,11},{8,4},{9,5},{10,6},{11,7},{20,24},{21,25... | collective-permute-start | bytes 1179656 | tf_op jit(solution)/shard_map/ppermute | solution.py:397
  83.5 18.0 %collective-permute-start.16 = (bf16[96,2048]{1,0:T(8,128)(2,1)S(1)}, bf16[96,2048]{1,0:T(8,128)(2,1)S(1)}, u32[]{:S(2)}, u32[]{:S(2)}) collective-permute-start(bf16[96,2048]{1,0:T(8,128)(2,1)S(1)} %collective-permute-done.12), channel_id=1, source_target_pairs={{4,0},{5,1},{6,2},{7,3},{8,12},{9,13},{10,14},{11,15},{20,16},{21,... | collective-permute-start | bytes 1179656 | tf_op jit(solution)/shard_map/ppermute | solution.py:400
  98.6 26.4 %collective-permute-start.7 = (bf16[96,2048]{1,0:T(8,128)(2,1)S(1)}, bf16[96,2048]{1,0:T(8,128)(2,1)S(1)}, u32[]{:S(2)}, u32[]{:S(2)}) collective-permute-start(bf16[96,2048]{1,0:T(8,128)(2,1)S(1)} %collective-permute-done.3), channel_id=1, source_target_pairs={{4,0},{5,1},{6,2},{7,3},{8,12},{9,13},{10,14},{11,15},{20,16},{21,... | collective-permute-start | bytes 1179656 | tf_op jit(solution)/shard_map/ppermute | solution.py:400
  100.1 24.9 %collective-permute-start.14 = (bf16[96,2048]{1,0:T(8,128)(2,1)S(1)}, bf16[96,2048]{1,0:T(8,128)(2,1)S(1)}, u32[]{:S(2)}, u32[]{:S(2)}) collective-permute-start(bf16[96,2048]{1,0:T(8,128)(2,1)S(1)} %collective-permute-done.13), channel_id=1, source_target_pairs={{4,0},{5,1},{6,2},{7,3},{8,12},{9,13},{10,14},{11,15},{20,16},{21,... | collective-permute-start | bytes 1179656 | tf_op jit(solution)/shard_map/ppermute | solution.py:399
  101.5 83.7 %collective-permute-start.34 = (bf16[32,32,768]{2,1,0:T(8,128)(2,1)}, bf16[32,32,768]{2,1,0:T(8,128)(2,1)}, u32[]{:S(2)}, u32[]{:S(2)}) collective-permute-start(bf16[32,32,768]{2,1,0:T(8,128)(2,1)} %shard_map.95.refs_8_), channel_id=1, source_target_pairs={{0,16},{16,0},{1,17},{17,1},{2,18},{18,2},{3,19},{19,3},{4,20},{20... | collective-permute-start | bytes 4718600 | tf_op jit(solution)/shard_map/ppermute | solution.py:441
  101.9 25.4 %collective-permute-start.18 = (bf16[96,1024]{1,0:T(8,128)(2,1)}, bf16[96,1024]{1,0:T(8,128)(2,1)S(1)}, u32[]{:S(2)}, u32[]{:S(2)}) collective-permute-start(bf16[96,1024]{1,0:T(8,128)(2,1)} %get-tuple-element.45), channel_id=1, source_target_pairs={{0,2},{1,3},{2,0},{3,1},{4,6},{5,7},{6,4},{7,5},{8,10},{9,11},{10,... | collective-permute-start | bytes 589832 | tf_op jit(solution)/shard_map/ppermute | solution.py:379
  127.4 22.6 %collective-permute-start.21 = (bf16[96,1024]{1,0:T(8,128)(2,1)}, bf16[96,1024]{1,0:T(8,128)(2,1)S(1)}, u32[]{:S(2)}, u32[]{:S(2)}) collective-permute-start(bf16[96,1024]{1,0:T(8,128)(2,1)} %get-tuple-element.51), channel_id=1, source_target_pairs={{0,8},{1,9},{2,10},{3,11},{4,12},{5,13},{6,14},{7,15},{8,0},{9,1},... | collective-permute-start | bytes 589832 | tf_op jit(solution)/shard_map/ppermute | solution.py:379
  135.7 19.2 %collective-permute-start.22 = (bf16[96,1024]{1,0:T(8,128)(2,1)}, bf16[96,1024]{1,0:T(8,128)(2,1)S(1)}, u32[]{:S(2)}, u32[]{:S(2)}) collective-permute-start(bf16[96,1024]{1,0:T(8,128)(2,1)} %get-tuple-element.53), channel_id=1, source_target_pairs={{0,10},{1,11},{2,8},{3,9},{4,14},{5,15},{6,12},{7,13},{8,2},{9,3},... | collective-permute-start | bytes 589832 | tf_op jit(solution)/shard_map/ppermute | solution.py:379
  155.6 20.0 %collective-permute-start.15 = (bf16[96,2048]{1,0:T(8,128)(2,1)S(1)}, bf16[96,2048]{1,0:T(8,128)(2,1)}, u32[]{:S(2)}, u32[]{:S(2)}) collective-permute-start(bf16[96,2048]{1,0:T(8,128)(2,1)S(1)} %broadcast_select_fusion.1.refs_4_.refs_12_), channel_id=1, source_target_pairs={{0,2},{1,3},{2,0},{3,1},{4,6},{5,7},{6,4},{7,5},{8,10},{9,11},{10,... | collective-permute-start | bytes 1179656 | tf_op jit(solution)/shard_map/ppermute | solution.py:379
  158.6 25.4 %collective-permute-start.17 = (bf16[96,2048]{1,0:T(8,128)(2,1)S(1)}, bf16[96,2048]{1,0:T(8,128)(2,1)}, u32[]{:S(2)}, u32[]{:S(2)}) collective-permute-start(bf16[96,2048]{1,0:T(8,128)(2,1)S(1)} %broadcast_select_fusion.refs_6_.refs_14_), channel_id=1, source_target_pairs={{0,2},{1,3},{2,0},{3,1},{4,6},{5,7},{6,4},{7,5},{8,10},{9,11},{10,... | collective-permute-start | bytes 1179656 | tf_op jit(solution)/shard_map/ppermute | solution.py:379
  167.2 32.4 %collective-permute-start.2 = (bf16[96,2048]{1,0:T(8,128)(2,1)S(1)}, bf16[96,2048]{1,0:T(8,128)(2,1)S(1)}, u32[]{:S(2)}, u32[]{:S(2)}) collective-permute-start(bf16[96,2048]{1,0:T(8,128)(2,1)S(1)} %copy-done.23), channel_id=1, source_target_pairs={{0,2},{1,3},{2,0},{3,1},{4,6},{5,7},{6,4},{7,5},{8,10},{9,11},{10,... | collective-permute-start | bytes 1179656 | tf_op jit(solution)/shard_map/ppermute | solution.py:379
  175.6 25.3 %collective-permute-start.6 = (bf16[96,2048]{1,0:T(8,128)(2,1)S(1)}, bf16[96,2048]{1,0:T(8,128)(2,1)}, u32[]{:S(2)}, u32[]{:S(2)}) collective-permute-start(bf16[96,2048]{1,0:T(8,128)(2,1)S(1)} %broadcast_select_fusion.3.refs_4_), channel_id=1, source_target_pairs={{0,2},{1,3},{2,0},{3,1},{4,6},{5,7},{6,4},{7,5},{8,10},{9,11},{10,... | collective-permute-start | bytes 1179656 | tf_op jit(solution)/shard_map/ppermute | solution.py:379
  184.0 22.6 %collective-permute-start.8 = (bf16[96,2048]{1,0:T(8,128)(2,1)S(1)}, bf16[96,2048]{1,0:T(8,128)(2,1)}, u32[]{:S(2)}, u32[]{:S(2)}) collective-permute-start(bf16[96,2048]{1,0:T(8,128)(2,1)S(1)} %broadcast_select_fusion.2.refs_6_), channel_id=1, source_target_pairs={{0,2},{1,3},{2,0},{3,1},{4,6},{5,7},{6,4},{7,5},{8,10},{9,11},{10,... | collective-permute-start | bytes 1179656 | tf_op jit(solution)/shard_map/ppermute | solution.py:379
  185.2 35.8 %collective-permute-start.25 = (bf16[32,32,768]{2,1,0:T(8,128)(2,1)}, bf16[32,32,768]{2,1,0:T(8,128)(2,1)S(1)}, u32[]{:S(2)}, u32[]{:S(2)}) collective-permute-start(bf16[32,32,768]{2,1,0:T(8,128)(2,1)} %shard_map.93.refs_16_), channel_id=1, source_target_pairs={{0,16},{16,0},{1,17},{17,1},{2,18},{18,2},{3,19},{19,3},{4,20},{20... | collective-permute-start | bytes 4718600 | tf_op jit(solution)/shard_map/ppermute | solution.py:441
  (44 other events, 1038.6 us)

commit v2 on v1

--- a/solution.py
+++ b/solution.py
@@ -16,9 +16,9 @@
 CHAIN = 4
 
 
-def params(n):
+def params(mebibytes):
     return pltpu.CompilerParams(
-        dimension_semantics=("arbitrary",) * n, vmem_limit_bytes=60 * 1024 * 1024
+        dimension_semantics=("arbitrary",), vmem_limit_bytes=mebibytes * 1024 * 1024
     )
 
 
@@ -86,7 +86,7 @@
         in_specs=[pl.BlockSpec((rows, d_tile, pairs), lambda i: (i, 0, 0))],
         out_specs=pl.BlockSpec((d_tile, rows, pairs), lambda i: (0, i, 0)),
         scratch_shapes=[pltpu.VMEM((TALL * d_tile, TALL * d_tile), BF16)],
-        compiler_params=params(1),
+        compiler_params=params(16),
         cost_estimate=pl.CostEstimate(
             flops=0, bytes_accessed=4 * doubles.size, transcendentals=0
         ),
@@ -131,7 +131,7 @@
                 pltpu.VMEM((TALL * a_rows, TALL * a_rows), BF16),
             ],
         ),
-        compiler_params=params(1),
+        compiler_params=params(60),
         cost_estimate=pl.CostEstimate(
             flops=2 * shard * a_rows * occ_rows * c_tile,
             bytes_accessed=10 * shard * a_rows * c_tile,
@@ -223,7 +223,7 @@
                 pltpu.VMEM((TALL * b_rows, TALL * b_rows), BF16),
             ],
         ),
-        compiler_params=params(1),
+        compiler_params=params(56),
         cost_estimate=pl.CostEstimate(
             flops=2 * shard * b_rows * occ_rows * wide,
             bytes_accessed=8 * shard * b_rows * wide,
@@ -265,7 +265,7 @@
         in_specs=[pl.BlockSpec((shard, width), lambda i: (0, i))] * slots,
         out_specs=pl.BlockSpec((d_tile, TALL, depth), lambda i: (0, i, 0)),
         scratch_shapes=[pltpu.VMEM((width, width), BF16)],
-        compiler_params=params(1),
+        compiler_params=params(16),
         cost_estimate=pl.CostEstimate(
             flops=0, bytes_accessed=4 * depth * columns, transcendentals=0
         ),
@@ -366,7 +366,7 @@
             pltpu.VMEM((rows, pairs), F32),
             pltpu.SemaphoreType.DMA((chunks * slots,)),
         ],
-        compiler_params=params(1),
+        compiler_params=params(28),
         cost_estimate=pl.CostEstimate(
             flops=2 * d_tile * 2 * b_local * columns * (depth + pairs),
             bytes_accessed=2 * depth * columns + 2 * doubles.size,
@@ -435,7 +435,7 @@
     for n, half in enumerate(halves):
         found = {0: half[0]}
         for slot in order:
-            gate = marks1["farthest"] if n else marks0["far"]
+            gate = marks1["farthest"] if n else marks0["far" if slot == 1 else "farthest"]
             found[slot] = exchange(gated(half[slot], gate), 2 * slot, size)
         own = turn([found[k] for k in range(slots)], d_tile)
         other = lax.ppermute(own, "col", [(0, 1), (1, 0)])

time: 268 us -> 246 us (0.918)
  Pallas kernels: 84.9 us -> 72.5 us
  waiting for transfers between devices: 122 us -> 117 us
  starting transfers between devices: 55.1 us -> 50.2 us
    ppermute x2, waiting for transfers between devices: 21.5 us -> 0.01 us  [plane_gather(): out_own = lax.ppermute(mid_own, 'dev', outward)]
    ppermute x25, waiting for transfers between devices: 88.5 us -> 99.5 us  [exchange(): return lax.ppermute(value, 'dev', [(d, d ^ bits) for d in range(size)])]
    pallas_call x3, Pallas kernels: 52.8 us -> 46.1 us  [ladder(): pl.pallas_call(functools.partial(ladder_kernel, slots, chunks, bool(start...]
    ppermute x2, waiting for transfers between devices: 0.01 us -> 5.48 us  [plane_gather(): out_near = lax.ppermute(mid_near, 'dev', outward)]
    pallas_call x2, Pallas kernels: 7.15 us -> 3.22 us  [turn(): pl.pallas_call(functools.partial(turn_kernel, slots, d_tile), out_shape=j...]
    ppermute x25, starting transfers between devices: 41.3 us -> 38.5 us  [exchange(): return lax.ppermute(value, 'dev', [(d, d ^ bits) for d in range(size)])]
  transfers between devices with their start and end apart: 37 -> 37, of which waited for: 20 -> 23; matrix products, arithmetic and copies ran while one was open for 0% -> 0% of each run, Pallas kernels for 20% -> 19%
where the time goes in v2:
time: 246 us; the launch traced here: 245 us
  waiting for transfers between devices  117 us (48%)
  Pallas kernels  72.5 us (29%)
  starting transfers between devices  50.2 us (20%)
  local copies, waits for them, and re-layouts  3.26 us (1%)
    ppermute x25, waiting for transfers between devices, exchange(): return lax.ppermute(value, 'dev', [(d, d ^ bits) for d in range(size)])  99.5 us
    pallas_call x3, Pallas kernels, ladder(): pl.pallas_call(functools.partial(ladder_kernel, slots, chunks, bool(start...  46.1 us
    ppermute x25, starting transfers between devices, exchange(): return lax.ppermute(value, 'dev', [(d, d ^ bits) for d in range(size)])  38.5 us
    pallas_call x1, Pallas kernels, dress_b(): pl.pallas_call(functools.partial(dress_b_kernel, slots), out_shape=[out]...  12 us
    all_to_all x1, waiting for transfers between devices, fast_body(): moved = lax.all_to_all(both, 'dev', split_axis=0, concat_axis=0, tiled=True)  10.2 us
    pallas_call x1, Pallas kernels, dress_a(): pl.pallas_call(dress_a_kernel, out_shape=[jax.ShapeDtypeStruct((shard, co...  6.69 us
    ppermute x2, waiting for transfers between devices, plane_gather(): out_near = lax.ppermute(mid_near, 'dev', outward)  5.48 us
  transfers between devices with their start and end apart: 37, of which 23 were waited for; matrix products, arithmetic and copies ran while one was open for 0% of the time, Pallas kernels for 19%

profile of v2, /device:TPU:0, one launch (start us, length us, event | category | flops | bytes accessed | tf_op | source)
XLA Modules:
  0.0 245.2 jit_solution(9730175802848616899)
XLA Ops:
  0.0 6.7 %shard_map.91 = (bf16[96,2048]{1,0:T(8,128)(2,1)}, bf16[96,2048]{1,0:T(8,128)(2,1)}) custom-call(s32[1]{0:T(128)} %bitcast.where, f32[1536,512]{1,0:T(8,128)} %bitcast.15, f32[1536,512]{1,0:T(8,128)} %bitcast.10, f32[16,16]{1,0:T(8,128)} %singles_ref.1), custom_call_target="tpu_custom_call" | custom-call | flops 12582912 | bytes 3932160 | tf_op jit(solution)/shard_map/pallas_call | solution.py:117
  10.4 8.6 %collective-permute-done.1.refs_2_ = bf16[96,2048]{1,0:T(8,128)(2,1)S(1)} collective-permute-done((bf16[96,2048]{1,0:T(8,128)(2,1)}, bf16[96,2048]{1,0:T(8,128)(2,1)S(1)}, u32[]{:S(2)}, u32[]{:S(2)}) %collective-permute-start.1) | collective-permute-done | bytes 393248 | tf_op jit(solution)/shard_map/ppermute | solution.py:379
  23.3 4.4 %shard_map.94.refs_10_ = bf16[32,256,256]{2,1,0:T(8,128)(2,1)} custom-call(bf16[256,32,256]{2,1,0:T(8,128)(2,1)S(1)} %copy-done), custom_call_target="tpu_custom_call" | custom-call | bytes 8388608 | tf_op jit(solution)/shard_map/pallas_call | solution.py:82
  29.4 12.0 %shard_map.92 = (bf16[96,1024]{1,0:T(8,128)(2,1)}, bf16[96,1024]{1,0:T(8,128)(2,1)}, bf16[96,1024]{1,0:T(8,128)(2,1)}, bf16[96,1024]{1,0:T(8,128)(2,1)}, bf16[96...) custom-call(s32[1]{0:T(128)} %bitcast.3.where, ...), custom_call_target="tpu_custom_call" | custom-call | flops 50331648 | bytes 12582912 | tf_op jit(solution)/shard_map/pallas_call | solution.py:211
  41.4 4.5 %collective-permute-start.10 = (bf16[96,2048]{1,0:T(8,128)(2,1)S(1)}, bf16[96,2048]{1,0:T(8,128)(2,1)S(1)}, u32[]{:S(2)}, u32[]{:S(2)}) collective-permute-start(bf16[96,2048]{1,0:T(8,128)(2,1)S(1)} %copy-done.4), channel_id=1, source_target_pairs={{0,4},{1,5},{2,6},{3,7},{4,0},{5,1},{6,2},{7,3},{8,12},{9,13},{10,... | collective-permute-start | bytes 1179656 | tf_op jit(solution)/shard_map/ppermute | solution.py:379
  49.5 6.3 %collective-permute-done.10.refs_2_.refs_10_ = bf16[96,2048]{1,0:T(8,128)(2,1)S(1)} collective-permute-done((bf16[96,2048]{1,0:T(8,128)(2,1)S(1)}, bf16[96,2048]{1,0:T(8,128)(2,1)S(1)}, u32[]{:S(2)}, u32[]{:S(2)}) %collective-permute-start.10) | collective-permute-done | bytes 393248 | tf_op jit(solution)/shard_map/ppermute | solution.py:379
  56.5 5.5 %collective-permute-done.7 = bf16[96,2048]{1,0:T(8,128)(2,1)S(1)} collective-permute-done((bf16[96,2048]{1,0:T(8,128)(2,1)S(1)}, bf16[96,2048]{1,0:T(8,128)(2,1)S(1)}, u32[]{:S(2)}, u32[]{:S(2)}) %collective-permute-start.7) | collective-permute-done | bytes 393248 | tf_op jit(solution)/shard_map/ppermute | solution.py:400
  67.2 7.4 %collective-permute-done.28.refs_2_ = bf16[96,1024]{1,0:T(8,128)(2,1)S(1)} collective-permute-done((bf16[96,1024]{1,0:T(8,128)(2,1)}, bf16[96,1024]{1,0:T(8,128)(2,1)S(1)}, u32[]{:S(2)}, u32[]{:S(2)}) %collective-permute-start.28) | collective-permute-done | bytes 196640 | tf_op jit(solution)/shard_map/ppermute | solution.py:379
  75.5 5.9 %collective-permute-done.29.refs_3_ = bf16[96,1024]{1,0:T(8,128)(2,1)S(1)} collective-permute-done((bf16[96,1024]{1,0:T(8,128)(2,1)}, bf16[96,1024]{1,0:T(8,128)(2,1)S(1)}, u32[]{:S(2)}, u32[]{:S(2)}) %collective-permute-start.29) | collective-permute-done | bytes 196640 | tf_op jit(solution)/shard_map/ppermute | solution.py:379
  88.7 4.2 %collective-permute-done.31.refs_5_ = bf16[96,1024]{1,0:T(8,128)(2,1)S(1)} collective-permute-done((bf16[96,1024]{1,0:T(8,128)(2,1)}, bf16[96,1024]{1,0:T(8,128)(2,1)S(1)}, u32[]{:S(2)}, u32[]{:S(2)}) %collective-permute-start.31) | collective-permute-done | bytes 196640 | tf_op jit(solution)/shard_map/ppermute | solution.py:379
  99.3 5.5 %collective-permute-done.refs_1_ = bf16[96,2048]{1,0:T(8,128)(2,1)S(1)} collective-permute-done((bf16[96,2048]{1,0:T(8,128)(2,1)S(1)}, bf16[96,2048]{1,0:T(8,128)(2,1)S(1)}, u32[]{:S(2)}, u32[]{:S(2)}) %collective-permute-start) | collective-permute-done | bytes 393248 | tf_op jit(solution)/shard_map/ppermute | solution.py:379
  106.4 6.9 %collective-permute-done.9.refs_1_.refs_9_ = bf16[96,2048]{1,0:T(8,128)(2,1)S(1)} collective-permute-done((bf16[96,2048]{1,0:T(8,128)(2,1)S(1)}, bf16[96,2048]{1,0:T(8,128)(2,1)S(1)}, u32[]{:S(2)}, u32[]{:S(2)}) %collective-permute-start.9) | collective-permute-done | bytes 393248 | tf_op jit(solution)/shard_map/ppermute | solution.py:379
  113.3 4.1 %collective-permute-start.19 = (bf16[96,1024]{1,0:T(8,128)(2,1)S(1)}, bf16[96,1024]{1,0:T(8,128)(2,1)S(1)}, u32[]{:S(2)}, u32[]{:S(2)}) collective-permute-start(bf16[96,1024]{1,0:T(8,128)(2,1)S(1)} %copy-done.13), channel_id=1, source_target_pairs={{0,4},{1,5},{2,6},{3,7},{4,0},{5,1},{6,2},{7,3},{8,12},{9,13},{10,... | collective-permute-start | bytes 589832 | tf_op jit(solution)/shard_map/ppermute | solution.py:379
  119.2 3.9 %collective-permute-done.19.refs_2_ = bf16[96,1024]{1,0:T(8,128)(2,1)S(1)} collective-permute-done((bf16[96,1024]{1,0:T(8,128)(2,1)S(1)}, bf16[96,1024]{1,0:T(8,128)(2,1)S(1)}, u32[]{:S(2)}, u32[]{:S(2)}) %collective-permute-start.19) | collective-permute-done | bytes 196640 | tf_op jit(solution)/shard_map/ppermute | solution.py:379
  123.1 3.7 %collective-permute-done.20.refs_3_ = bf16[96,1024]{1,0:T(8,128)(2,1)S(1)} collective-permute-done((bf16[96,1024]{1,0:T(8,128)(2,1)S(1)}, bf16[96,1024]{1,0:T(8,128)(2,1)S(1)}, u32[]{:S(2)}, u32[]{:S(2)}) %collective-permute-start.20) | collective-permute-done | bytes 196640 | tf_op jit(solution)/shard_map/ppermute | solution.py:379
  126.8 10.9 %collective-permute-done.21.refs_4_ = bf16[96,1024]{1,0:T(8,128)(2,1)S(1)} collective-permute-done((bf16[96,1024]{1,0:T(8,128)(2,1)S(1)}, bf16[96,1024]{1,0:T(8,128)(2,1)S(1)}, u32[]{:S(2)}, u32[]{:S(2)}) %collective-permute-start.21) | collective-permute-done | bytes 196640 | tf_op jit(solution)/shard_map/ppermute | solution.py:379
  149.6 5.5 %collective-permute-done.11.refs_3_.refs_11_ = bf16[96,2048]{1,0:T(8,128)(2,1)S(1)} collective-permute-done((bf16[96,2048]{1,0:T(8,128)(2,1)S(1)}, bf16[96,2048]{1,0:T(8,128)(2,1)S(1)}, u32[]{:S(2)}, u32[]{:S(2)}) %collective-permute-start.11) | collective-permute-done | bytes 393248 | tf_op jit(solution)/shard_map/ppermute | solution.py:379
  156.4 7.2 %collective-permute-done.15.refs_5_.refs_13_ = bf16[96,2048]{1,0:T(8,128)(2,1)S(1)} collective-permute-done((bf16[96,2048]{1,0:T(8,128)(2,1)S(1)}, bf16[96,2048]{1,0:T(8,128)(2,1)S(1)}, u32[]{:S(2)}, u32[]{:S(2)}) %collective-permute-start.15) | collective-permute-done | bytes 393248 | tf_op jit(solution)/shard_map/ppermute | solution.py:379
  164.8 7.2 %collective-permute-done.17.refs_7_.refs_15_ = bf16[96,2048]{1,0:T(8,128)(2,1)S(1)} collective-permute-done((bf16[96,2048]{1,0:T(8,128)(2,1)S(1)}, bf16[96,2048]{1,0:T(8,128)(2,1)S(1)}, u32[]{:S(2)}, u32[]{:S(2)}) %collective-permute-start.17) | collective-permute-done | bytes 393248 | tf_op jit(solution)/shard_map/ppermute | solution.py:379
  173.2 12.9 %shard_map.97.refs_20_ = f32[512,256]{1,0:T(8,128)S(1)} custom-call(bf16[96,2048]{1,0:T(8,128)(2,1)S(1)} %copy-done.4, bf16[96,2048]{1,0:T(8,128)(2,1)S(1)} %collective-permute-done.9.refs_1_.refs_9_, bf16[96,2048]{1,0:T(8,128)(2,1)S(1)} %collective-permute-done.10.refs_2_.refs_10_, bf16[96,2048]{1,0:T(8,128)(2,1)S(1)} %collective-permute-done.11.refs_3_.refs_11_, ...), custom_call_target="tpu_custom_call" | custom-call | flops 8589934592 | bytes 7340032 | tf_op jit(solution)/shard_map/pallas_call | solution.py:354
  188.8 5.6 %collective-permute-done.8.refs_7_ = bf16[96,2048]{1,0:T(8,128)(2,1)S(1)} collective-permute-done((bf16[96,2048]{1,0:T(8,128)(2,1)S(1)}, bf16[96,2048]{1,0:T(8,128)(2,1)S(1)}, u32[]{:S(2)}, u32[]{:S(2)}) %collective-permute-start.8) | collective-permute-done | bytes 393248 | tf_op jit(solution)/shard_map/ppermute | solution.py:379
  194.4 12.9 %shard_map.96.refs_19_ = f32[512,256]{1,0:T(8,128)S(1)} custom-call(bf16[96,2048]{1,0:T(8,128)(2,1)S(1)} %copy-done.3, bf16[96,2048]{1,0:T(8,128)(2,1)S(1)} %collective-permute-done.refs_1_, bf16[96,2048]{1,0:T(8,128)(2,1)S(1)} %collective-permute-done.1.refs_2_, bf16[96,2048]{1,0:T(8,128)(2,1)S(1)} %collective-permute-done.2.refs_3_, ...), custom_call_target="tpu_custom_call" | custom-call | flops 8589934592 | bytes 7340032 | tf_op jit(solution)/shard_map/pallas_call | solution.py:354
  207.4 20.2 %shard_map.98 = (f32[2,8,32,256]{3,2,1,0:T(8,128)S(1)}, f32[2,8,32,256]{3,2,1,0:T(8,128)S(1)}) custom-call(bf16[96,2048]{1,0:T(8,128)(2,1)S(1)} %copy-done.3, bf16[96,2048]{1,0:T(8,128)(2,1)S(1)} %collective-permute-done.refs_1_, bf16[96,2048]{1,0:T(8,128)(2,1)S(1)} %collective-permute-done.1.refs_2_, bf16[96,2048]{1,0:T(8,128)(2,1)S(1)} %collective-permute-done.2.refs_3_, ...), custom_call_target="tpu_custom_call" | custom-call | flops 17179869184 | bytes 10485760 | tf_op jit(solution)/shard_map/pallas_call | solution.py:354
  234.3 10.2 %all-to-all-done = bf16[16,32,256]{2,1,0:T(8,128)(2,1)S(1)} async-done(((bf16[16,32,256]{2,1,0:T(8,128)(2,1)}), bf16[16,32,256]{2,1,0:T(8,128)(2,1)S(1)}, u32[]{:S(2)}, u32[]{:S(2)}) %all-to-all-start) | async-done | bytes 262176 | tf_op jit(solution)/shard_map/all_to_all | solution.py:451
  (100 shorter events, 62.4 us)
Async XLA Ops:
  19.1 27.5 %collective-permute-start.3 = (bf16[96,2048]{1,0:T(8,128)(2,1)S(1)}, bf16[96,2048]{1,0:T(8,128)(2,1)S(1)}, u32[]{:S(2)}, u32[]{:S(2)}) collective-permute-start(bf16[96,2048]{1,0:T(8,128)(2,1)S(1)} %collective-permute-done.1.refs_2_), channel_id=1, source_target_pairs={{4,8},{5,9},{6,10},{7,11},{8,4},{9,5},{10,6},{11,7},{20,24},{21,25... | collective-permute-start | bytes 1179656 | tf_op jit(solution)/shard_map/ppermute | solution.py:398
  19.8 28.1 %collective-permute-start.5 = (bf16[96,2048]{1,0:T(8,128)(2,1)S(1)}, bf16[96,2048]{1,0:T(8,128)(2,1)S(1)}, u32[]{:S(2)}, u32[]{:S(2)}) collective-permute-start(bf16[96,2048]{1,0:T(8,128)(2,1)S(1)} %collective-permute-done.4), channel_id=1, source_target_pairs={{4,0},{5,1},{6,2},{7,3},{8,12},{9,13},{10,14},{11,15},{20,16},{21,... | collective-permute-start | bytes 1179656 | tf_op jit(solution)/shard_map/ppermute | solution.py:399
  27.7 179.7 %collective-permute-start.26 = (bf16[32,256,256]{2,1,0:T(8,128)(2,1)}, bf16[32,256,256]{2,1,0:T(8,128)(2,1)}, u32[]{:S(2)}, u32[]{:S(2)}) collective-permute-start(bf16[32,256,256]{2,1,0:T(8,128)(2,1)} %shard_map.94.refs_10_), channel_id=1, source_target_pairs={{0,1},{1,0},{2,3},{3,2},{4,5},{5,4},{6,7},{7,6},{8,9},{9,8},{10,11... | collective-permute-start | bytes 12582920 | tf_op jit(solution)/shard_map/ppermute | solution.py:379
  41.4 14.4 %collective-permute-start.10 = (bf16[96,2048]{1,0:T(8,128)(2,1)S(1)}, bf16[96,2048]{1,0:T(8,128)(2,1)S(1)}, u32[]{:S(2)}, u32[]{:S(2)}) collective-permute-start(bf16[96,2048]{1,0:T(8,128)(2,1)S(1)} %copy-done.4), channel_id=1, source_target_pairs={{0,4},{1,5},{2,6},{3,7},{4,0},{5,1},{6,2},{7,3},{8,12},{9,13},{10,... | collective-permute-start | bytes 1179656 | tf_op jit(solution)/shard_map/ppermute | solution.py:379
  45.9 16.3 %collective-permute-start.13 = (bf16[96,2048]{1,0:T(8,128)(2,1)S(1)}, bf16[96,2048]{1,0:T(8,128)(2,1)S(1)}, u32[]{:S(2)}, u32[]{:S(2)}) collective-permute-start(bf16[96,2048]{1,0:T(8,128)(2,1)S(1)} %copy-done.4), channel_id=1, source_target_pairs={{4,8},{5,9},{6,10},{7,11},{8,4},{9,5},{10,6},{11,7},{20,24},{21,25... | collective-permute-start | bytes 1179656 | tf_op jit(solution)/shard_map/ppermute | solution.py:397
  46.6 15.4 %collective-permute-start.7 = (bf16[96,2048]{1,0:T(8,128)(2,1)S(1)}, bf16[96,2048]{1,0:T(8,128)(2,1)S(1)}, u32[]{:S(2)}, u32[]{:S(2)}) collective-permute-start(bf16[96,2048]{1,0:T(8,128)(2,1)S(1)} %collective-permute-done.3), channel_id=1, source_target_pairs={{4,0},{5,1},{6,2},{7,3},{8,12},{9,13},{10,14},{11,15},{20,16},{21,... | collective-permute-start | bytes 1179656 | tf_op jit(solution)/shard_map/ppermute | solution.py:400
  48.0 17.2 %collective-permute-start.27 = (bf16[96,1024]{1,0:T(8,128)(2,1)}, bf16[96,1024]{1,0:T(8,128)(2,1)S(1)}, u32[]{:S(2)}, u32[]{:S(2)}) collective-permute-start(bf16[96,1024]{1,0:T(8,128)(2,1)} %get-tuple-element.60), channel_id=1, source_target_pairs={{0,2},{1,3},{2,0},{3,1},{4,6},{5,7},{6,4},{7,5},{8,10},{9,11},{10,... | collective-permute-start | bytes 589832 | tf_op jit(solution)/shard_map/ppermute | solution.py:379
  62.1 19.3 %collective-permute-start.29 = (bf16[96,1024]{1,0:T(8,128)(2,1)}, bf16[96,1024]{1,0:T(8,128)(2,1)S(1)}, u32[]{:S(2)}, u32[]{:S(2)}) collective-permute-start(bf16[96,1024]{1,0:T(8,128)(2,1)} %get-tuple-element.64), channel_id=1, source_target_pairs={{0,6},{1,7},{2,4},{3,5},{4,2},{5,3},{6,0},{7,1},{8,14},{9,15},{10,... | collective-permute-start | bytes 589832 | tf_op jit(solution)/shard_map/ppermute | solution.py:379
  65.1 21.4 %collective-permute-start.30 = (bf16[96,1024]{1,0:T(8,128)(2,1)}, bf16[96,1024]{1,0:T(8,128)(2,1)S(1)}, u32[]{:S(2)}, u32[]{:S(2)}) collective-permute-start(bf16[96,1024]{1,0:T(8,128)(2,1)} %get-tuple-element.66), channel_id=1, source_target_pairs={{0,8},{1,9},{2,10},{3,11},{4,12},{5,13},{6,14},{7,15},{8,0},{9,1},... | collective-permute-start | bytes 589832 | tf_op jit(solution)/shard_map/ppermute | solution.py:379
  65.9 33.3 %collective-permute-start.16 = (bf16[96,2048]{1,0:T(8,128)(2,1)S(1)}, bf16[96,2048]{1,0:T(8,128)(2,1)S(1)}, u32[]{:S(2)}, u32[]{:S(2)}) collective-permute-start(bf16[96,2048]{1,0:T(8,128)(2,1)S(1)} %collective-permute-done.12), channel_id=1, source_target_pairs={{4,0},{5,1},{6,2},{7,3},{8,12},{9,13},{10,14},{11,15},{20,16},{21,... | collective-permute-start | bytes 1179656 | tf_op jit(solution)/shard_map/ppermute | solution.py:400
  74.6 18.3 %collective-permute-start.31 = (bf16[96,1024]{1,0:T(8,128)(2,1)}, bf16[96,1024]{1,0:T(8,128)(2,1)S(1)}, u32[]{:S(2)}, u32[]{:S(2)}) collective-permute-start(bf16[96,1024]{1,0:T(8,128)(2,1)} %get-tuple-element.68), channel_id=1, source_target_pairs={{0,10},{1,11},{2,8},{3,9},{4,14},{5,15},{6,12},{7,13},{8,2},{9,3},... | collective-permute-start | bytes 589832 | tf_op jit(solution)/shard_map/ppermute | solution.py:379
  94.3 19.0 %collective-permute-start.9 = (bf16[96,2048]{1,0:T(8,128)(2,1)S(1)}, bf16[96,2048]{1,0:T(8,128)(2,1)S(1)}, u32[]{:S(2)}, u32[]{:S(2)}) collective-permute-start(bf16[96,2048]{1,0:T(8,128)(2,1)S(1)} %copy-done.4), channel_id=1, source_target_pairs={{0,2},{1,3},{2,0},{3,1},{4,6},{5,7},{6,4},{7,5},{8,10},{9,11},{10,... | collective-permute-start | bytes 1179656 | tf_op jit(solution)/shard_map/ppermute | solution.py:379
  95.2 22.1 %collective-permute-start.14 = (bf16[96,2048]{1,0:T(8,128)(2,1)S(1)}, bf16[96,2048]{1,0:T(8,128)(2,1)S(1)}, u32[]{:S(2)}, u32[]{:S(2)}) collective-permute-start(bf16[96,2048]{1,0:T(8,128)(2,1)S(1)} %collective-permute-done.13), channel_id=1, source_target_pairs={{4,0},{5,1},{6,2},{7,3},{8,12},{9,13},{10,14},{11,15},{20,16},{21,... | collective-permute-start | bytes 1179656 | tf_op jit(solution)/shard_map/ppermute | solution.py:399
  99.2 74.0 %collective-permute-start.34 = (bf16[32,32,768]{2,1,0:T(8,128)(2,1)S(1)}, bf16[32,32,768]{2,1,0:T(8,128)(2,1)S(1)}, u32[]{:S(2)}, u32[]{:S(2)}) collective-permute-start(bf16[32,32,768]{2,1,0:T(8,128)(2,1)S(1)} %shard_map.95.refs_8_), channel_id=1, source_target_pairs={{0,16},{16,0},{1,17},{17,1},{2,18},{18,2},{3,19},{19,3},{4,20},{20... | collective-permute-start | bytes 4718600 | tf_op jit(solution)/shard_map/ppermute | solution.py:441
  117.5 20.3 %collective-permute-start.21 = (bf16[96,1024]{1,0:T(8,128)(2,1)S(1)}, bf16[96,1024]{1,0:T(8,128)(2,1)S(1)}, u32[]{:S(2)}, u32[]{:S(2)}) collective-permute-start(bf16[96,1024]{1,0:T(8,128)(2,1)S(1)} %copy-done.11), channel_id=1, source_target_pairs={{0,8},{1,9},{2,10},{3,11},{4,12},{5,13},{6,14},{7,15},{8,0},{9,1},... | collective-permute-start | bytes 589832 | tf_op jit(solution)/shard_map/ppermute | solution.py:379
  123.1 20.0 %collective-permute-start.22 = (bf16[96,1024]{1,0:T(8,128)(2,1)S(1)}, bf16[96,1024]{1,0:T(8,128)(2,1)S(1)}, u32[]{:S(2)}, u32[]{:S(2)}) collective-permute-start(bf16[96,1024]{1,0:T(8,128)(2,1)S(1)} %copy-done.10), channel_id=1, source_target_pairs={{0,10},{1,11},{2,8},{3,9},{4,14},{5,15},{6,12},{7,13},{8,2},{9,3},... | collective-permute-start | bytes 589832 | tf_op jit(solution)/shard_map/ppermute | solution.py:379
  126.8 16.6 %collective-permute-start.23 = (bf16[96,1024]{1,0:T(8,128)(2,1)S(1)}, bf16[96,1024]{1,0:T(8,128)(2,1)S(1)}, u32[]{:S(2)}, u32[]{:S(2)}) collective-permute-start(bf16[96,1024]{1,0:T(8,128)(2,1)S(1)} %copy-done.9), channel_id=1, source_target_pairs={{0,12},{1,13},{2,14},{3,15},{4,8},{5,9},{6,10},{7,11},{8,4},{9,5},... | collective-permute-start | bytes 589832 | tf_op jit(solution)/shard_map/ppermute | solution.py:379
  143.4 20.1 %collective-permute-start.15 = (bf16[96,2048]{1,0:T(8,128)(2,1)S(1)}, bf16[96,2048]{1,0:T(8,128)(2,1)S(1)}, u32[]{:S(2)}, u32[]{:S(2)}) collective-permute-start(bf16[96,2048]{1,0:T(8,128)(2,1)S(1)} %broadcast_select_fusion.1.refs_4_.refs_12_), channel_id=1, source_target_pairs={{0,2},{1,3},{2,0},{3,1},{4,6},{5,7},{6,4},{7,5},{8,10},{9,11},{10,... | collective-permute-start | bytes 1179656 | tf_op jit(solution)/shard_map/ppermute | solution.py:379
  146.2 25.7 %collective-permute-start.17 = (bf16[96,2048]{1,0:T(8,128)(2,1)S(1)}, bf16[96,2048]{1,0:T(8,128)(2,1)S(1)}, u32[]{:S(2)}, u32[]{:S(2)}) collective-permute-start(bf16[96,2048]{1,0:T(8,128)(2,1)S(1)} %broadcast_select_fusion.refs_6_.refs_14_), channel_id=1, source_target_pairs={{0,2},{1,3},{2,0},{3,1},{4,6},{5,7},{6,4},{7,5},{8,10},{9,11},{10,... | collective-permute-start | bytes 1179656 | tf_op jit(solution)/shard_map/ppermute | solution.py:379
  155.1 31.1 %collective-permute-start.2 = (bf16[96,2048]{1,0:T(8,128)(2,1)S(1)}, bf16[96,2048]{1,0:T(8,128)(2,1)S(1)}, u32[]{:S(2)}, u32[]{:S(2)}) collective-permute-start(bf16[96,2048]{1,0:T(8,128)(2,1)S(1)} %collective-permute-done.1.refs_2_), channel_id=1, source_target_pairs={{0,2},{1,3},{2,0},{3,1},{4,6},{5,7},{6,4},{7,5},{8,10},{9,11},{10,... | collective-permute-start | bytes 1179656 | tf_op jit(solution)/shard_map/ppermute | solution.py:379
  163.5 25.3 %collective-permute-start.6 = (bf16[96,2048]{1,0:T(8,128)(2,1)S(1)}, bf16[96,2048]{1,0:T(8,128)(2,1)S(1)}, u32[]{:S(2)}, u32[]{:S(2)}) collective-permute-start(bf16[96,2048]{1,0:T(8,128)(2,1)S(1)} %broadcast_select_fusion.3.refs_4_), channel_id=1, source_target_pairs={{0,2},{1,3},{2,0},{3,1},{4,6},{5,7},{6,4},{7,5},{8,10},{9,11},{10,... | collective-permute-start | bytes 1179656 | tf_op jit(solution)/shard_map/ppermute | solution.py:379
  171.9 22.5 %collective-permute-start.8 = (bf16[96,2048]{1,0:T(8,128)(2,1)S(1)}, bf16[96,2048]{1,0:T(8,128)(2,1)S(1)}, u32[]{:S(2)}, u32[]{:S(2)}) collective-permute-start(bf16[96,2048]{1,0:T(8,128)(2,1)S(1)} %broadcast_select_fusion.2.refs_6_), channel_id=1, source_target_pairs={{0,2},{1,3},{2,0},{3,1},{4,6},{5,7},{6,4},{7,5},{8,10},{9,11},{10,... | collective-permute-start | bytes 1179656 | tf_op jit(solution)/shard_map/ppermute | solution.py:379
  173.2 34.2 %collective-permute-start.25 = (bf16[32,32,768]{2,1,0:T(8,128)(2,1)S(1)}, bf16[32,32,768]{2,1,0:T(8,128)(2,1)S(1)}, u32[]{:S(2)}, u32[]{:S(2)}) collective-permute-start(bf16[32,32,768]{2,1,0:T(8,128)(2,1)S(1)} %shard_map.93.refs_16_), channel_id=1, source_target_pairs={{0,16},{16,0},{1,17},{17,1},{2,18},{18,2},{3,19},{19,3},{4,20},{20... | collective-permute-start | bytes 4718600 | tf_op jit(solution)/shard_map/ppermute | solution.py:441
  230.5 13.9 %all-to-all-start = ((bf16[16,32,256]{2,1,0:T(8,128)(2,1)}), bf16[16,32,256]{2,1,0:T(8,128)(2,1)S(1)}, u32[]{:S(2)}, u32[]{:S(2)}) async-start(bf16[16,32,256]{2,1,0:T(8,128)(2,1)} %bitcast.5), calls=%async_computation | async-start | bytes 524288 | tf_op jit(solution)/shard_map/all_to_all | solution.py:451
  (28 other events, 942.6 us)
